TPU v7x, 32 devices: a whole 2x2x4 slice. The times are simulated.
32 devices in a mesh: seq: 4 (over y, core), mp: 8 (over z, x).
Axes of the slice: x: 2, y: 2, z: 4, core: 2. Of those that a mesh axis runs over, the one named last changes fastest.
Arguments:
- inputs: bfloat16 [8, 1024, 2048], P('mp', 'seq'), may hold values from -6 to 6
- cotangent: bfloat16 [8, 1024, 2048], P('mp', 'seq'), may hold values from -6 to 6
- segment_ids: int32 [8, 1024], P('mp', 'seq'), may hold values from 0 to 3, never falling along the last dimension, each value on 1 to 512 neighbouring positions
- mixer_gain: bfloat16 [2048], P('mp'), may hold values from 0.5 to 1.5
- query_weight: bfloat16 [2048, 2048], P(None, 'mp'), may hold values from -0.125 to 0.125
- key_weight: bfloat16 [2048, 2048], P(None, 'mp'), may hold values from -0.125 to 0.125
- value_weight: bfloat16 [2048, 2048], P(None, 'mp'), may hold values from -0.125 to 0.125
- swish_weight: bfloat16 [2048, 2048], P(None, 'mp'), may hold values from -0.125 to 0.125
- decay_weight: bfloat16 [2048, 16], P('mp'), may hold values from -0.25 to 0.25
- decay_bias: float32 [16], replicated, may hold values from -1 to 7
- output_weight: bfloat16 [2048, 2048], P('mp'), may hold values from -0.25 to 0.25
- feed_gain: bfloat16 [2048], P('mp'), may hold values from 0.5 to 1.5
- gate_weight: bfloat16 [2048, 5504], P(None, 'mp'), may hold values from -0.125 to 0.125
- up_weight: bfloat16 [2048, 5504], P(None, 'mp'), may hold values from -0.125 to 0.125
- down_weight: bfloat16 [5504, 2048], P('mp'), may hold values from -0.15625 to 0.15625
Outputs:
- layer_out: bfloat16 [8, 1024, 2048], P('mp', 'seq')
- input_grad: bfloat16 [8, 1024, 2048], P('mp', 'seq')
- mixer_grad: float32 [2048], P('mp')
- query_grad: float32 [2048, 2048], P(None, 'mp')
- key_grad: float32 [2048, 2048], P(None, 'mp')
- value_grad: float32 [2048, 2048], P(None, 'mp')
- swish_grad: float32 [2048, 2048], P(None, 'mp')
- decay_grad: float32 [2048, 16], P('mp')
- bias_grad: float32 [16], replicated
- output_grad: float32 [2048, 2048], P('mp')
- feed_grad: float32 [2048], P('mp')
- gate_grad: float32 [2048, 5504], P(None, 'mp')
- up_grad: float32 [2048, 5504], P(None, 'mp')
- down_grad: float32 [5504, 2048], P('mp')
Inputs may be any that keep to these rules, and one draw needn't show every extreme that they name: `segment_ids`: within each sequence the ids never fall; each document spans 1 to 512 tokens, and one spans exactly that many.
All inputs are finite; a program needn't handle non-finite values.
Results may differ from a plain program's by a relative error of at most 0.025.
Values may be sent and summed in bfloat16 or wider, within the bound.
No kernel may reach another device: no remote copies, remote signals or barrier semaphores. Data moves between devices by JAX's collectives and lax.ppermute only.
A program may use at most 384 MiB of HBM per device.

v0:
```python
from functools import partial

import jax
import jax.numpy as jnp
from jax import lax
from jax.sharding import PartitionSpec as P

highest = lax.Precision.HIGHEST
rms_eps = 1e-06
group_eps = 16.0


def prefix(shard, axis, combine, identity):
    length, place = (lax.axis_size(axis), lax.axis_index(axis))
    everything = jax.tree.map(
        lambda part, kind: lax.all_gather(part.astype(kind), axis),
        shard,
        (jnp.bfloat16, jnp.bfloat16),
    )
    start = jax.tree.map(
        lambda part, zero: jnp.broadcast_to(jnp.asarray(zero, part.dtype), part.shape),
        shard,
        identity,
    )

    def prefix_hop(k, before):
        reached = k < place
        new = combine(
            before, jax.tree.map(lambda part, own: part[k].astype(own.dtype), everything, shard)
        )
        return jax.tree.map(lambda a, b: jnp.where(reached, a, b), new, before)

    return lax.fori_loop(0, length, prefix_hop, start)


def carried_in(shard, axis, combine, identity):
    length, place = (lax.axis_size(axis), lax.axis_index(axis))
    everything = jax.tree.map(
        lambda part, kind: lax.all_gather(part.astype(kind), axis),
        shard,
        jax.tree.map(lambda a: jnp.bfloat16 if a.dtype == jnp.float32 else a.dtype, shard),
    )
    start = jax.tree.map(
        lambda part, zero: jnp.broadcast_to(jnp.asarray(zero, part.dtype), part.shape),
        shard,
        identity,
    )

    def carried_hop(k, before):
        at = length - 1 - k
        reached = at > place
        new = combine(
            before, jax.tree.map(lambda part, own: part[at].astype(own.dtype), everything, shard)
        )
        return jax.tree.map(lambda a, b: jnp.where(reached, a, b), new, before)

    return lax.fori_loop(0, length, carried_hop, start)


def passed_along(value, axis, steps):
    count = lax.axis_size(axis)
    first, last = (max(0, -steps), min(count, count - steps))
    return lax.ppermute(value, axis, [(source, source + steps) for source in range(first, last)])


def local_out(queries, key_rows, values, decays, incoming, segment, previous):
    cumulative = jnp.cumsum(decays, axis=0)
    length_rows = segment.shape[0]
    positions = jnp.arange(length_rows)
    causal = (positions[:, None] >= positions[None, :]) & (segment[:, None] == segment[None, :])
    differ = cumulative.T[:, :, None] - cumulative.T[:, None, :]
    weights = jnp.where(causal[None], jnp.exp(jnp.minimum(differ, 0.0)), 0.0)
    scores = jnp.einsum("thd,shd->hts", queries, key_rows, precision=highest) * weights
    outputs = jnp.einsum("hts,she->the", scores, values, precision=highest)
    entry_decay = jnp.exp(cumulative) * (segment == previous)[:, None].astype(cumulative.dtype)
    return outputs + entry_decay[:, :, None] * jnp.einsum(
        "thd,hde->the", queries, incoming, precision=highest
    )


def local_tail(key_rows, values, decays, segment, previous):
    cumulative = jnp.cumsum(decays, axis=0)
    last_index = segment.shape[0] - 1
    last_id = segment[last_index]
    final_sum = cumulative[last_index]
    carry_keep = jnp.exp(final_sum) * (last_id == previous).astype(cumulative.dtype)
    tail_decay = jnp.exp(final_sum[None, :] - cumulative) * (segment == last_id)[:, None].astype(
        cumulative.dtype
    )
    tail_states = jnp.einsum(
        "shd,she->hde", key_rows * tail_decay[:, :, None], values, precision=highest
    )
    return (carry_keep, tail_states)


def out_batch(queries, key_rows, values, decays, incoming, segment, previous):
    return jax.vmap(local_out)(queries, key_rows, values, decays, incoming, segment, previous)


def tail_batch(key_rows, values, decays, segment, previous):
    return jax.vmap(local_tail)(key_rows, values, decays, segment, previous)


def compose(earlier, latter):
    return (earlier[0] * latter[0], latter[0][..., None, None] * earlier[1] + latter[1])


def scan_states(keep_part, state_part, identity):
    return prefix((keep_part, state_part), "seq", compose, identity)[1]


def scan_grads(keep_part, grad_part, identity):
    return carried_in((keep_part, grad_part), "seq", compose, identity)[1]


def silu_slope(pre_act):
    logistic = jax.nn.sigmoid(pre_act)
    return logistic * (1.0 + pre_act * (1.0 - logistic))


def rms_back(grad_normed, source, scaling, gain_row):
    base_part = source * scaling
    scaled_grad = grad_normed * gain_row
    gain_part = jnp.sum(grad_normed * base_part, axis=0)
    source_grad = scaling * (
        scaled_grad - base_part * jnp.mean(scaled_grad * base_part, axis=-1, keepdims=True)
    )
    return (gain_part, source_grad)


def left_dot(left_side, right_side):
    return lax.dot_general(
        left_side, right_side, (((0,), (0,)), ((), ())), preferred_element_type=jnp.float32
    )


def right_dot(left_side, right_side):
    return lax.dot_general(
        left_side, right_side, (((1,), (1,)), ((), ())), preferred_element_type=jnp.float32
    )


def tensor_body(
    inputs,
    cotangent,
    segment_ids,
    previous_piece,
    mixer_gain,
    query_weight,
    key_weight,
    value_weight,
    swish_weight,
    decay_weight,
    decay_bias,
    output_weight,
    feed_gain,
    gate_weight,
    up_weight,
    down_weight,
):
    model_ways = lax.axis_size("mp")
    rank = lax.axis_index("mp")
    tokens = inputs[0].astype(jnp.float32)
    length_rows = tokens.shape[0]
    width = tokens.shape[1]
    heads = decay_bias.shape[0]
    head_size = width // heads
    local_width = query_weight.shape[1]
    local_heads = local_width // head_size
    params = (
        lax.all_gather(mixer_gain, "mp", axis=0, tiled=True),
        lax.all_gather(feed_gain, "mp", axis=0, tiled=True),
        lax.all_gather(decay_weight, "mp", axis=0, tiled=True),
    )
    gain_one = params[0].astype(jnp.float32)
    gain_two = params[1].astype(jnp.float32)
    decay_cols = lax.dynamic_slice_in_dim(params[2], rank * local_heads, local_heads, 1)
    bias_cols = lax.dynamic_slice_in_dim(decay_bias, rank * local_heads, local_heads, 0)
    id_set = (
        lax.all_gather(segment_ids, "mp", axis=0, tiled=True),
        lax.all_gather(previous_piece, "mp", axis=0, tiled=True),
    )
    segments = id_set[0]
    previous_all = id_set[1]
    scale_one = lax.rsqrt(jnp.mean(tokens * tokens, axis=-1, keepdims=True) + rms_eps)
    normed = (tokens * scale_one * gain_one).astype(jnp.bfloat16)
    rows = (
        lax.all_gather(normed[None], "mp", axis=0, tiled=True),
        lax.all_gather(cotangent, "mp", axis=0, tiled=True),
    )
    groups = rows[0].shape[0]
    flat = groups * length_rows
    normed_all = rows[0].reshape(flat, width)
    grad_out_all = rows[1].reshape(flat, width)
    queries = jnp.dot(normed_all, query_weight, preferred_element_type=jnp.float32).astype(
        jnp.bfloat16
    )
    key_rows = jnp.dot(normed_all, key_weight, preferred_element_type=jnp.float32).astype(
        jnp.bfloat16
    )
    values = jnp.dot(normed_all, value_weight, preferred_element_type=jnp.float32).astype(
        jnp.bfloat16
    )
    swish_pre = jnp.dot(normed_all, swish_weight, preferred_element_type=jnp.float32)
    decay_pre = jnp.dot(normed_all, decay_cols, preferred_element_type=jnp.float32) + bias_cols
    decays = -jax.nn.softplus(-decay_pre) / 16.0
    shaped = (groups, length_rows, local_heads, head_size)
    query_heads = queries.astype(jnp.float32).reshape(shaped)
    key_heads = key_rows.astype(jnp.float32).reshape(shaped)
    value_heads = values.astype(jnp.float32).reshape(shaped)
    decay_heads = decays.reshape(groups, length_rows, local_heads)
    tail_pair, tail_pullback = jax.vjp(
        partial(tail_batch, segment=segments, previous=previous_all),
        key_heads,
        value_heads,
        decay_heads,
    )
    identity = (
        jnp.ones((groups, local_heads), jnp.float32),
        jnp.zeros((groups, local_heads, head_size, head_size), jnp.float32),
    )
    incoming = scan_states(tail_pair[0], tail_pair[1], identity)
    outputs, out_pullback = jax.vjp(
        partial(out_batch, segment=segments, previous=previous_all),
        query_heads,
        key_heads,
        value_heads,
        decay_heads,
        incoming,
    )
    centered = outputs - jnp.mean(outputs, axis=-1, keepdims=True)
    inverse = lax.rsqrt(jnp.mean(centered * centered, axis=-1, keepdims=True) + group_eps)
    normed_heads = centered * inverse
    swish = jax.nn.silu(swish_pre)
    gated = (normed_heads.reshape(flat, local_width) * swish).astype(jnp.bfloat16)
    attn_part = jnp.dot(gated, output_weight, preferred_element_type=jnp.float32)
    attended = lax.psum_scatter(
        attn_part.reshape(groups, length_rows, width).astype(jnp.bfloat16),
        "mp",
        scatter_dimension=0,
        tiled=True,
    ).astype(jnp.float32)[0]
    mixed = tokens + attended
    scale_two = lax.rsqrt(jnp.mean(mixed * mixed, axis=-1, keepdims=True) + rms_eps)
    normed_two = (mixed * scale_two * gain_two).astype(jnp.bfloat16)
    two_rows = lax.all_gather(normed_two[None], "mp", axis=0, tiled=True).reshape(flat, width)
    gate_pre = jnp.dot(two_rows, gate_weight, preferred_element_type=jnp.float32)
    up_pre = jnp.dot(two_rows, up_weight, preferred_element_type=jnp.float32)
    hidden = (jax.nn.silu(gate_pre) * up_pre).astype(jnp.bfloat16)
    down_part = jnp.dot(hidden, down_weight, preferred_element_type=jnp.float32)
    result = (
        mixed
        + lax.psum_scatter(
            down_part.reshape(groups, length_rows, width).astype(jnp.bfloat16),
            "mp",
            scatter_dimension=0,
            tiled=True,
        ).astype(jnp.float32)[0]
    )
    layer_out = result.astype(jnp.bfloat16)[None]
    down_local = left_dot(hidden, grad_out_all)
    grad_hidden = right_dot(grad_out_all, down_weight)
    grad_gate = (grad_hidden * up_pre * silu_slope(gate_pre)).astype(jnp.bfloat16)
    grad_up = (grad_hidden * jax.nn.silu(gate_pre)).astype(jnp.bfloat16)
    gate_local = left_dot(two_rows, grad_gate)
    up_local = left_dot(two_rows, grad_up)
    two_part = right_dot(grad_gate, gate_weight) + right_dot(grad_up, up_weight)
    grad_normed_two = lax.psum_scatter(
        two_part.reshape(groups, length_rows, width).astype(jnp.bfloat16),
        "mp",
        scatter_dimension=0,
        tiled=True,
    ).astype(jnp.float32)[0]
    feed_gain_full, grad_mixed_part = rms_back(grad_normed_two, mixed, scale_two, gain_two)
    grad_mixed = cotangent[0].astype(jnp.float32) + grad_mixed_part
    grad_attended = grad_mixed.astype(jnp.bfloat16)
    attended_rows = lax.all_gather(grad_attended[None], "mp", axis=0, tiled=True).reshape(
        flat, width
    )
    output_local = left_dot(gated, attended_rows)
    grad_gated = right_dot(attended_rows, output_weight)
    grad_swish = (
        grad_gated * normed_heads.reshape(flat, local_width) * silu_slope(swish_pre)
    ).astype(jnp.bfloat16)
    grad_grouped = (grad_gated * swish).reshape(shaped)
    grad_heads = inverse * (
        grad_grouped
        - jnp.mean(grad_grouped, axis=-1, keepdims=True)
        - normed_heads * jnp.mean(grad_grouped * normed_heads, axis=-1, keepdims=True)
    )
    cumulative = jnp.cumsum(decay_heads, axis=1)
    entry_decay = jnp.exp(cumulative) * (segments == previous_all[:, None])[:, :, None].astype(
        jnp.float32
    )
    own_grad = jnp.einsum(
        "bthd,bthe->bhde", query_heads * entry_decay[..., None], grad_heads, precision=highest
    )
    later_grad = scan_grads(tail_pair[0], own_grad, identity)
    grad_query, grad_key, grad_value, grad_decay, grad_entry = out_pullback(grad_heads)
    keep_cot = jnp.sum(later_grad * incoming, axis=(-2, -1))
    tail_key, tail_value, tail_decay = tail_pullback((keep_cot, later_grad))
    query_low = grad_query.reshape(flat, local_width).astype(jnp.bfloat16)
    key_low = (grad_key + tail_key).reshape(flat, local_width).astype(jnp.bfloat16)
    value_low = (grad_value + tail_value).reshape(flat, local_width).astype(jnp.bfloat16)
    decay_pre_grad = (
        (grad_decay + tail_decay).reshape(flat, local_heads) * jax.nn.sigmoid(-decay_pre) / 16.0
    )
    bias_local = jnp.sum(decay_pre_grad, axis=0)
    decay_low = decay_pre_grad.astype(jnp.bfloat16)
    query_local = left_dot(normed_all, query_low)
    key_local = left_dot(normed_all, key_low)
    value_local = left_dot(normed_all, value_low)
    swish_local = left_dot(normed_all, grad_swish)
    decay_local = left_dot(normed_all, decay_low)
    normed_part = (
        right_dot(query_low, query_weight)
        + right_dot(key_low, key_weight)
        + right_dot(value_low, value_weight)
        + right_dot(grad_swish, swish_weight)
        + right_dot(decay_low, decay_cols)
    )
    grad_normed = lax.psum_scatter(
        normed_part.reshape(groups, length_rows, width).astype(jnp.bfloat16),
        "mp",
        scatter_dimension=0,
        tiled=True,
    ).astype(jnp.float32)[0]
    mixer_gain_full, grad_tokens_part = rms_back(grad_normed, tokens, scale_one, gain_one)
    input_grad = (grad_mixed + grad_tokens_part).astype(jnp.bfloat16)[None]
    decay_tile = lax.dynamic_update_slice_in_dim(
        jnp.zeros((width, heads), jnp.float32), decay_local, rank * local_heads, 1
    )
    bias_pad = lax.dynamic_update_slice_in_dim(
        jnp.zeros((heads,), jnp.float32), bias_local, rank * local_heads, 0
    )
    bias_tile = jnp.broadcast_to(bias_pad[None, :], (model_ways, heads))
    owned = (
        lax.psum_scatter(
            mixer_gain_full.astype(jnp.bfloat16), "mp", scatter_dimension=0, tiled=True
        ).astype(jnp.float32),
        lax.psum_scatter(
            feed_gain_full.astype(jnp.bfloat16), "mp", scatter_dimension=0, tiled=True
        ).astype(jnp.float32),
        lax.psum_scatter(
            decay_tile.astype(jnp.bfloat16), "mp", scatter_dimension=0, tiled=True
        ).astype(jnp.float32),
        lax.psum_scatter(
            bias_tile.astype(jnp.bfloat16), "mp", scatter_dimension=0, tiled=True
        ).astype(jnp.float32),
    )
    totals = (
        lax.psum(owned[0].astype(jnp.bfloat16), "seq").astype(jnp.float32),
        lax.psum(query_local.astype(jnp.bfloat16), "seq").astype(jnp.float32),
        lax.psum(key_local.astype(jnp.bfloat16), "seq").astype(jnp.float32),
        lax.psum(value_local.astype(jnp.bfloat16), "seq").astype(jnp.float32),
        lax.psum(swish_local.astype(jnp.bfloat16), "seq").astype(jnp.float32),
        lax.psum(owned[2].astype(jnp.bfloat16), "seq").astype(jnp.float32),
        lax.psum(owned[3].astype(jnp.bfloat16), "seq").astype(jnp.float32),
        lax.psum(output_local.astype(jnp.bfloat16), "seq").astype(jnp.float32),
        lax.psum(owned[1].astype(jnp.bfloat16), "seq").astype(jnp.float32),
        lax.psum(gate_local.astype(jnp.bfloat16), "seq").astype(jnp.float32),
        lax.psum(up_local.astype(jnp.bfloat16), "seq").astype(jnp.float32),
        lax.psum(down_local.astype(jnp.bfloat16), "seq").astype(jnp.float32),
    )
    return (
        layer_out,
        input_grad,
        totals[0],
        totals[1],
        totals[2],
        totals[3],
        totals[4],
        totals[5],
        totals[6].reshape(heads),
        totals[7],
        totals[8],
        totals[9],
        totals[10],
        totals[11],
    )


def per_device(
    inputs,
    cotangent,
    segment_ids,
    mixer_gain,
    query_weight,
    key_weight,
    value_weight,
    swish_weight,
    decay_weight,
    decay_bias,
    output_weight,
    feed_gain,
    gate_weight,
    up_weight,
    down_weight,
):
    length_rows = inputs.shape[1]
    previous_piece = passed_along(segment_ids[0][length_rows - 1 :], "seq", 1)
    return tensor_body(
        inputs,
        cotangent,
        segment_ids,
        previous_piece,
        mixer_gain,
        query_weight,
        key_weight,
        value_weight,
        swish_weight,
        decay_weight,
        decay_bias,
        output_weight,
        feed_gain,
        gate_weight,
        up_weight,
        down_weight,
    )


def solution(mesh):
    placed = (
        P("mp", "seq", None),
        P("mp", "seq", None),
        P("mp", "seq"),
        P("mp"),
        P(None, "mp"),
        P(None, "mp"),
        P(None, "mp"),
        P(None, "mp"),
        P("mp", None),
        P(),
        P("mp", None),
        P("mp"),
        P(None, "mp"),
        P(None, "mp"),
        P("mp", None),
    )
    return jax.shard_map(
        per_device,
        mesh=mesh,
        in_specs=placed,
        out_specs=(
            P("mp", "seq", None),
            P("mp", "seq", None),
            P("mp"),
            P(None, "mp"),
            P(None, "mp"),
            P(None, "mp"),
            P(None, "mp"),
            P("mp", None),
            P(),
            P("mp", None),
            P("mp"),
            P(None, "mp"),
            P(None, "mp"),
            P("mp", None),
        ),
        check_vma=False,
    )
```

profile of v0, /device:TPU:1, one launch (start us, length us, event | category | flops | bytes accessed | tf_op | source)
XLA Modules:
  0.0 1722.8 jit_solution(11767068099736795838)
XLA Ops:
  9.7 17.9 %all-gather.2 = bf16[8,1,256]{2,1,0:T(2,128)(2,1)S(1)} all-gather(bf16[1,1,256]{2,1,0:T(2,128)(2,1)S(1)} %reshape.456), channel_id=1, replica_groups=mesh['seq'=4,'mp'=8] {'mp'}, dimensions={0}, use_global_device_ids=true | all-gather | bytes 4608 | tf_op jit(solution)/shard_map/all_gather | solution.py:171
  31.3 7.5 collective-permute-start
  38.8 13.2 all-gather.3
  52.7 24.8 %all_gather.48 = bf16[2048,16]{0,1:T(8,128)(2,1)S(1)} all-gather(bf16[256,16]{0,1:T(8,128)(2,1)S(1)} %copy-done.71), channel_id=1, replica_groups=mesh['seq'=4,'mp'=8] {'mp'}, dimensions={0}, use_global_device_ids=true | all-gather | bytes 73728 | tf_op jit(solution)/shard_map/all_gather | solution.py:173
  79.2 6.5 all-reduce.1
  86.7 70.4 %all-gather.12.cloned.1.call-done = bf16[8,256,2048]{2,1,0:T(8,128)(2,1)} async-done(((bf16[1,256,2048]{2,1,0:T(8,128)(2,1)}), bf16[8,256,2048]{2,1,0:T(8,128)(2,1)}) %all-gather.12.cloned.1.call-update) | async-done | bytes 8388624 | tf_op jit(solution)/shard_map/all_gather | solution.py:188
  157.1 6.3 fusion.113
  168.1 6.9 convolution_convert_fusion.10
  177.2 6.9 convolution_convert_fusion.12
  192.4 6.3 all_gather.50
  198.8 7.0 convolution_convert_fusion.11
  215.9 10.3 while.30
  241.5 8.4 fusion.44
  256.2 14.6 all-gather.4
  270.7 132.5 %reduce-scatter.6.cloned.1.call-done = bf16[1,256,2048]{2,1,0:T(8,128)(2,1)} async-done(((bf16[8,256,2048]{2,1,0:T(8,128)(2,1)}), bf16[1,256,2048]{2,1,0:T(8,128)(2,1)}) %reduce-scatter.6.cloned.1.call-update) | async-done | bytes 1048592 | tf_op jit(solution)/shard_map/reduce_scatter | solution.py:237
  407.6 123.0 %all-gather.14.cloned.1.call-done = bf16[8,256,2048]{2,1,0:T(8,128)(2,1)} async-done(((bf16[1,256,2048]{2,1,0:T(8,128)(2,1)}), bf16[8,256,2048]{2,1,0:T(8,128)(2,1)}) %all-gather.14.cloned.1.call-update) | async-done | bytes 8388624 | tf_op jit(solution)/shard_map/all_gather | solution.py:246
  530.6 11.1 fusion.138
  541.7 7.8 fusion.137
  549.5 106.4 %all-gather.16.cloned.1.call-done = bf16[8,256,2048]{2,1,0:T(8,128)(2,1)} async-done(((bf16[1,256,2048]{2,1,0:T(8,128)(2,1)}), bf16[8,256,2048]{2,1,0:T(8,128)(2,1)}) %all-gather.16.cloned.1.call-update) | async-done | bytes 8388624 | tf_op jit(solution)/shard_map/all_gather | solution.py:189
  655.9 14.1 multiply_convert_fusion
  670.0 10.7 fusion.139
  680.8 12.6 add_convert_fusion.1
  693.4 147.7 %reduce-scatter.10.cloned.1.call-done = bf16[1,256,2048]{2,1,0:T(8,128)(2,1)} async-done(((bf16[8,256,2048]{2,1,0:T(8,128)(2,1)}), bf16[1,256,2048]{2,1,0:T(8,128)(2,1)}) %reduce-scatter.10.cloned.1.call-update) | async-done | bytes 1048592 | tf_op jit(solution)/shard_map/reduce_scatter | solution.py:268
  848.6 10.5 convolution_convert_fusion.2
  859.1 10.8 convolution_convert_fusion.3
  869.9 7.4 convolution_convert_fusion.4
  877.3 94.8 %all-gather.18.cloned.1.call-done = bf16[8,256,2048]{2,1,0:T(8,128)(2,1)} async-done(((bf16[1,256,2048]{2,1,0:T(8,128)(2,1)}), bf16[8,256,2048]{2,1,0:T(8,128)(2,1)}) %all-gather.18.cloned.1.call-update) | async-done | bytes 8388624 | tf_op jit(solution)/shard_map/all_gather | solution.py:277
  972.1 9.7 fusion.46
  1006.2 7.9 fusion.131
  1040.4 8.0 fusion.12
  1048.4 6.9 convolution_convert_fusion.5
  1062.6 12.9 while.31
  1084.0 5.9 fusion.48
  1094.0 7.3 convolution_convert_fusion.8
  1101.3 6.9 convolution_convert_fusion.7
  1108.6 10.3 fusion.140
  1127.0 9.1 fusion.116
  1136.1 8.2 fusion.142
  1144.3 8.2 fusion.141
  1152.5 27.4 %add_convert_fusion = bf16[2048,2048]{1,0:T(8,128)(2,1)} fusion(f32[2048,2048]{1,0:T(8,128)} %fusion.116, f32[2048,2048]{1,0:T(8,128)} %fusion.142, f32[2048,2048]{1,0:T(8,128)} %fusion.140, f32[2048,2048]{1,0:T(8,128)} %fusion.141, bf16[2048,256]{1,0:T(8,128)(2,1)} %get-tuple-element.326, bf16[2048,256]{1,0:T(8,128)(2,1)} %param.26), kind=kOutput, calls=%fused_computation.6 | convolution fusion | flops 2168455168 | bytes 77594624 | tf_op jit(solution)/shard_map/dot_general | solution.py:138
  1185.4 11.2 convolution_convert_fusion
  1197.5 150.5 %all-reduce.10.cloned.1.call-done = (bf16[2048,256]{1,0:T(8,128)(2,1)}, bf16[2048,256]{1,0:T(8,128)(2,1)}, bf16[2048,256]{1,0:T(8,128)(2,1)}, bf16[2048,256]{1,0...) async-done(((bf16[2048,256]{1,0:T(8,128)(2,1)}, bf16[2048,256]{1,0:T(8,128)(2,1)}, ...) | async-done | bytes 13697040 | tf_op jit(solution)/shard_map/psum | solution.py:353
  1366.8 134.1 %reduce-scatter.12.cloned.1.call-done = bf16[1,256,2048]{2,1,0:T(8,128)(2,1)} async-done(((bf16[8,256,2048]{2,1,0:T(8,128)(2,1)}), bf16[1,256,2048]{2,1,0:T(8,128)(2,1)}) %reduce-scatter.12.cloned.1.call-update) | async-done | bytes 1048592 | tf_op jit(solution)/shard_map/reduce_scatter | solution.py:322
  1503.4 28.2 %all-reduce.5 = (bf16[2048]{0:T(1024)(128)(2,1)S(1)}, bf16[8,16]{1,0:T(8,128)(2,1)S(1)}, bf16[2048]{0:T(1024)(128)(2,1)S(1)}) all-reduce(bf16[2048]{0:T(1024)(128)(2,1)S(1)} %get-tuple-element.282, bf16[8,16]{1,0:T(8,128)(2,1)S(1)} %broadcast_in_dim.34, bf16[2048]{0:T(1024)(128)(2,1)S(1)} %copy-done.66), channel_id=8, replica_groups=mesh['seq'=4,'mp'=8] {'mp'}, use_global_device_ids=true, to_apply=%region_29.30.clone | all-reduce | flops 4224 | bytes 16896
  1532.4 23.0 %reduce-scatter.14.cloned.1.call-done = bf16[256,16]{0,1:T(8,128)(2,1)} async-done(((bf16[2048,16]{0,1:T(8,128)(2,1)}), bf16[256,16]{0,1:T(8,128)(2,1)}) %reduce-scatter.14.cloned.1.call-update) | async-done | bytes 8208 | tf_op jit(solution)/shard_map/reduce_scatter | solution.py:344
  1555.4 8.2 all-reduce.6
  1565.9 143.8 %reduce-scatter.8.cloned.1.call-done = bf16[1,256,2048]{2,1,0:T(8,128)(2,1)} async-done(((bf16[8,256,2048]{2,1,0:T(8,128)(2,1)}), bf16[1,256,2048]{2,1,0:T(8,128)(2,1)}) %reduce-scatter.8.cloned.1.call-update) | async-done | bytes 1048592 | tf_op jit(solution)/shard_map/reduce_scatter | solution.py:253
  1709.7 5.8 fusion.33
  (361 shorter events, 199.9 us)
Async XLA Ops:
  7.2 648.7 %copy-start = (bf16[688,2048]{1,0:T(8,128)(2,1)S(1)}, bf16[688,2048]{1,0:T(8,128)(2,1)}, u32[]{:S(2)}) copy-start(bf16[688,2048]{1,0:T(8,128)(2,1)} %param.33) | copy-start | bytes 8454148
  7.2 44.8 %copy-start.72 = (u32[32]{0:T(128)S(1)}, u32[32]{0:T(128)}, u32[]{:S(2)}) copy-start(u32[32]{0:T(128)} %constant.139) | copy-start | bytes 388
  7.2 23.5 %copy-start.75 = (s32[1,256]{1,0:T(1,128)S(1)}, s32[1,256]{1,0:T(1,128)}, u32[]{:S(2)}) copy-start(s32[1,256]{1,0:T(1,128)} %param.21) | copy-start | bytes 3076
  7.2 45.5 %copy-start.71 = (bf16[256,16]{0,1:T(8,128)(2,1)S(1)}, bf16[256,16]{0,1:T(8,128)(2,1)}, u32[]{:S(2)}) copy-start(bf16[256,16]{0,1:T(8,128)(2,1)} %param.27) | copy-start | bytes 24580
  7.2 71.9 %copy-start.80 = (f32[16]{0:T(128)S(1)}, f32[16]{0:T(128)}, u32[]{:S(2)}) copy-start(f32[16]{0:T(128)} %param.28) | copy-start | bytes 196
  7.2 149.9 %all-gather.12.cloned.1.call-start = ((), (), s32[]{:S(2)}) async-start(), calls=%async_computation.5 | async-start | bytes 9437184 | tf_op jit(solution)/shard_map/all_gather | solution.py:188
  9.6 17.9 %copy-start.67 = (f32[256]{0:T(256)}, f32[256]{0:T(256)S(1)}, u32[]{:S(2)}) copy-start(f32[256]{0:T(256)S(1)} %add_rsqrt_fusion.2) | copy-start | bytes 3076
  30.7 185.2 %all-gather.20.cloned.1.call-start = ((), (), s32[]{:S(2)}) async-start(), calls=%async_computation.14 | async-start | bytes 2621440 | tf_op jit(solution)/shard_map/all_gather | solution.py:16
  31.3 46.4 %collective-permute-start = (s32[1]{0:T(128)}, s32[1]{0:T(128)}, u32[]{:S(2)}, u32[]{:S(2)}) collective-permute-start(s32[1]{0:T(128)} %bitcast.8), channel_id=1, source_target_pairs={{0,8},{8,16},{16,24},{1,9},{9,17},{17,25},{2,10},{10,18},{18,26},{... | collective-permute-start | bytes 20 | tf_op jit(solution)/shard_map/ppermute | solution.py:63
  77.5 85.9 %copy-start.53 = (bf16[2048,16]{0,1:T(8,128)(2,1)}, bf16[2048,16]{0,1:T(8,128)(2,1)S(1)}, u32[]{:S(2)}) copy-start(bf16[2048,16]{0,1:T(8,128)(2,1)S(1)} %all_gather.48) | copy-start | bytes 196612
  85.7 71.4 %copy-start.55 = (f32[8,256]{1,0:T(8,128)}, f32[8,256]{1,0:T(8,128)S(1)}, u32[]{:S(2)}) copy-start(f32[8,256]{1,0:T(8,128)S(1)} %get-tuple-element.333) | copy-start | bytes 24580
  85.7 71.4 %copy-start.57 = (f32[8,256]{1,0:T(8,128)}, f32[8,256]{1,0:T(8,128)S(1)}, u32[]{:S(2)}) copy-start(f32[8,256]{1,0:T(8,128)S(1)} %get-tuple-element.332) | copy-start | bytes 24580
  165.0 27.4 %copy-start.23 = (f32[8,2,256]{0,1,2:T(2,128)}, f32[8,2,256]{0,1,2:T(2,128)S(1)}, u32[]{:S(2)}) copy-start(f32[8,2,256]{0,1,2:T(2,128)S(1)} %copy.277) | copy-start | bytes 49156
  168.1 18.2 %copy-start.59 = (f32[8,256,2]{1,2,0:T(2,128)}, f32[8,256,2]{1,2,0:T(2,128)S(1)}, u32[]{:S(2)}) copy-start(f32[8,256,2]{1,2,0:T(2,128)S(1)} %copy.282) | copy-start | bytes 49156
  191.1 212.2 %reduce-scatter.6.cloned.1.call-start = ((), (), s32[]{:S(2)}) async-start(), calls=%async_computation.6 | async-start | bytes 9437184 | tf_op jit(solution)/shard_map/reduce_scatter | solution.py:237
  192.4 13.4 copy-start.73
  198.7 30.2 %copy-start.49 = (f32[8,2,256]{2,1,0:T(2,128)}, f32[8,2,256]{2,1,0:T(2,128)S(1)}, u32[]{:S(2)}) copy-start(f32[8,2,256]{2,1,0:T(2,128)S(1)} %copy.274) | copy-start | bytes 49156
  198.8 30.1 %copy-start.47 = (f32[8,256,2]{1,2,0:T(2,128)}, f32[8,256,2]{1,2,0:T(2,128)S(1)}, u32[]{:S(2)}) copy-start(f32[8,256,2]{1,2,0:T(2,128)S(1)} %copy.279) | copy-start | bytes 49156
  215.9 13.0 copy-start.33
  255.5 275.0 %all-gather.14.cloned.1.call-start = ((), (), s32[]{:S(2)}) async-start(), calls=%async_computation.7 | async-start | bytes 9437184 | tf_op jit(solution)/shard_map/all_gather | solution.py:246
  270.7 573.9 %copy-start.45 = (f32[8,1,256]{2,1,0:T(1,128)}, f32[8,1,256]{2,1,0:T(1,128)S(1)}, u32[]{:S(2)}) copy-start(f32[8,1,256]{2,1,0:T(1,128)S(1)} %convert_element_type.376) | copy-start | bytes 24580
  405.4 439.3 %copy-start.61 = (f32[256]{0:T(256)}, f32[256]{0:T(256)S(1)}, u32[]{:S(2)}) copy-start(f32[256]{0:T(256)S(1)} %add_rsqrt_fusion.1) | copy-start | bytes 3076
  406.9 249.0 %all-gather.16.cloned.1.call-start = ((), (), s32[]{:S(2)}) async-start(), calls=%async_computation.9 | async-start | bytes 9437184 | tf_op jit(solution)/shard_map/all_gather | solution.py:189
  407.5 433.6 %reduce-scatter.10.cloned.1.call-start = ((), (), s32[]{:S(2)}) async-start(), calls=%async_computation.10 | async-start | bytes 9437184 | tf_op jit(solution)/shard_map/reduce_scatter | solution.py:268
  530.5 11.2 copy-start.76
  530.5 11.2 copy-start.77
  655.9 14.1 copy-start.78
  670.0 10.7 copy-start.84
  670.0 10.7 copy-start.83
  670.0 10.8 copy-start.79
  693.4 278.8 %all-gather.18.cloned.1.call-start = ((), (), s32[]{:S(2)}) async-start(), calls=%async_computation.11 | async-start | bytes 9437184 | tf_op jit(solution)/shard_map/all_gather | solution.py:277
  848.5 214.1 %all-gather.22.cloned.1.call-start = ((), (), s32[]{:S(2)}) async-start(), calls=%async_computation.15 | async-start | bytes 2621440 | tf_op jit(solution)/shard_map/all_gather | solution.py:39
  848.6 21.3 %slice-start.2 = ((s8[8388608]{0:T(1024)(128)(4,1)}), s8[4194304]{0:T(1024)(128)(4,1)S(1)}, s32[]{:S(2)}) async-start(s8[8388608]{0:T(1024)(128)(4,1)} %bitcast.352), calls=%async_computation.19 | async-start | bytes 8388608
  859.1 10.8 slice-start.3
  859.1 10.8 copy-start.86
  1014.1 333.8 %all-reduce.10.cloned.1.call-start = ((), (), s32[]{:S(2)}) async-start(), calls=%async_computation.16 | async-start | bytes 27394048 | tf_op jit(solution)/shard_map/psum | solution.py:353
  1040.4 14.9 slice-start
  1108.2 10.9 copy-start.56
  1108.3 11.1 copy-start.65
  1108.3 392.7 %reduce-scatter.12.cloned.1.call-start = ((), (), s32[]{:S(2)}) async-start(), calls=%async_computation.12 | async-start | bytes 9437184 | tf_op jit(solution)/shard_map/reduce_scatter | solution.py:322
  1179.9 375.5 %reduce-scatter.14.cloned.1.call-start = ((), (), s32[]{:S(2)}) async-start(), calls=%async_computation.13 | async-start | bytes 73728 | tf_op jit(solution)/shard_map/reduce_scatter | solution.py:344
  1185.3 524.4 %reduce-scatter.8.cloned.1.call-start = ((), (), s32[]{:S(2)}) async-start(), calls=%async_computation.8 | async-start | bytes 9437184 | tf_op jit(solution)/shard_map/reduce_scatter | solution.py:253
  1363.5 137.4 %copy-start.52 = (f32[8,1,256]{2,1,0:T(1,128)S(1)}, f32[8,1,256]{2,1,0:T(1,128)}, u32[]{:S(2)}) copy-start(f32[8,1,256]{2,1,0:T(1,128)} %copy-done.51) | copy-start | bytes 24580
  1363.5 137.4 %copy-start.68 = (f32[256]{0:T(256)S(1)}, f32[256]{0:T(256)}, u32[]{:S(2)}) copy-start(f32[256]{0:T(256)} %copy-done.67) | copy-start | bytes 3076
  1363.5 139.8 %copy-start.66 = (bf16[2048]{0:T(1024)(128)(2,1)S(1)}, bf16[2048]{0:T(1024)(128)(2,1)}, u32[]{:S(2)}) copy-start(bf16[2048]{0:T(1024)(128)(2,1)} %get-tuple-element.280) | copy-start | bytes 12292
  1363.6 346.2 %copy-start.46 = (f32[8,1,256]{2,1,0:T(1,128)S(1)}, f32[8,1,256]{2,1,0:T(1,128)}, u32[]{:S(2)}) copy-start(f32[8,1,256]{2,1,0:T(1,128)} %copy-done.45) | copy-start | bytes 24580
  1363.6 346.2 %copy-start.62 = (f32[256]{0:T(256)S(1)}, f32[256]{0:T(256)}, u32[]{:S(2)}) copy-start(f32[256]{0:T(256)} %copy-done.61) | copy-start | bytes 3076
  1363.6 346.2 %copy-start.70 = (f32[256]{0:T(256)S(1)}, f32[256]{0:T(256)}, u32[]{:S(2)}) copy-start(f32[256]{0:T(256)} %copy-done.69) | copy-start | bytes 3076
  (56 other events, 261.0 us)
Sparse Core Ops, SparseCore 0:
  30.8 126.2 all-gather.11
  191.2 21.5 all-gather.19
  255.6 147.5 reduce-scatter.5
  407.0 123.4 all-gather.13
  532.7 123.1 all-gather.15
  693.5 147.6 reduce-scatter.9
  848.6 123.4 all-gather.17
  1014.2 21.5 all-gather.21
  1108.4 239.5 all-reduce.9
  1351.4 149.4 reduce-scatter.11
  1505.0 50.4 reduce-scatter.13
  1559.3 150.3 reduce-scatter.7
where the time goes:
time: 1730 us; the launch traced here: 1720 us
  waiting for transfers between devices  1130 us (65%)
  matrix products  302 us (17%)
  blocking collectives  120 us (7%)
  other arithmetic  97 us (6%)
  local copies, waits for them, and re-layouts  52.3 us (3%)
    psum x1, waiting for transfers between devices, tensor_body(): lax.psum(query_local.astype(jnp.bfloat16), 'seq').astype(jnp.float32)  150 us
    reduce_scatter x1, waiting for transfers between devices, tensor_body(): lax.psum_scatter(two_part.reshape(groups, length_rows, width).astype(jnp....  148 us
    reduce_scatter x1, waiting for transfers between devices, tensor_body(): lax.psum_scatter(down_part.reshape(groups, length_rows, width).astype(jnp...  144 us
    reduce_scatter x1, waiting for transfers between devices, tensor_body(): lax.psum_scatter(normed_part.reshape(groups, length_rows, width).astype(j...  134 us
    reduce_scatter x1, waiting for transfers between devices, tensor_body(): lax.psum_scatter(attn_part.reshape(groups, length_rows, width).astype(jnp...  133 us
    all_gather x1, waiting for transfers between devices, tensor_body(): lax.all_gather(normed_two[None], 'mp', axis=0, tiled=True)  123 us
    dot_general x9, matrix products, right_dot(): lax.dot_general(left_side, right_side, (((1,), (1,)), ((), ())), preferre...  110 us
    all_gather x1, waiting for transfers between devices, tensor_body(): lax.all_gather(cotangent, 'mp', axis=0, tiled=True)  106 us
  transfers between devices with their start and end apart: 13, of which 10 were waited for; matrix products, arithmetic and copies ran while one was open for 13% of the time, Pallas kernels for 0%

commit v1 on v0

v1 whole, which is shorter than its diff:
```python
import jax
import jax.numpy as jnp
from jax import lax
from jax.experimental import pallas as pl
from jax.experimental.pallas import tpu as pltpu
from jax.sharding import PartitionSpec as P

rms_eps = 1e-06
group_eps = 16.0
f32 = jnp.float32
bf16 = jnp.bfloat16


def dot(left, right, dims, **kw):
    return lax.dot_general(
        left, right, ((dims[0], dims[1]), ((), ())), preferred_element_type=f32, **kw
    )


def mm(left, right):
    return dot(left, right, ((1,), (0,)))


def mm_t(left, right):
    return dot(left, right, ((1,), (1,)))


def t_mm(left, right):
    return dot(left, right, ((0,), (0,)))


def silu_slope(pre_act):
    logistic = jax.nn.sigmoid(pre_act)
    return logistic * (1.0 + pre_act * (1.0 - logistic))


class Place:
    def __init__(self):
        self.seq_ways, self.ways = lax.axis_size("seq"), lax.axis_size("mp")
        seat = lax.axis_index("seq")
        self.rank = lax.axis_index("mp")
        self.row, self.core = seat >> 1, seat & 1
        self.rows = self.seq_ways // 2
        self.side = self.row & 1
        self.top = self.ways // 2
        self.lows = [1 << b for b in range(self.ways.bit_length() - 2) if (1 << b) != 2]

    def hop(self, value, where):
        pairs = []
        for seat in range(self.seq_ways):
            for rank in range(self.ways):
                to = where(seat // 2, seat % 2, rank)
                if to is not None:
                    pairs.append((seat * self.ways + rank, (to[0] * 2 + to[1]) * self.ways + to[2]))
        return lax.ppermute(value, ("seq", "mp"), pairs)

    def other_core(self, value):
        return self.hop(value, lambda y, c, m: (y, 1 - c, m))

    def partner(self, value):
        return self.hop(value, lambda y, c, m: (y, c, m ^ 2))

    def over(self, value, bit):
        return self.hop(value, lambda y, c, m: (y, c, m ^ bit))


def halves(value, axis):
    size = value.shape[axis] // 2
    return (
        lax.slice_in_dim(value, 0, size, axis=axis),
        lax.slice_in_dim(value, size, 2 * size, axis=axis),
    )


def pick(flag, first, second):
    return jnp.where(flag == 0, first, second)


def after(value, *tokens):
    tokens = [t for t in tokens if t is not None]
    return lax.optimization_barrier((value, *tokens))[0] if tokens else value


def joined(at, got, other, axis):
    return jnp.concatenate([pick(at.side, got, other), pick(at.side, other, got)], axis=axis)


def gather_weight(at, weight, axis, shared):
    low, high = halves(weight, axis)
    got = at.hop(
        pick(at.side, low, high), lambda y, c, m: (y, c, m ^ at.top) if c == 1 else None
    )
    other = at.hop(got, lambda y, c, m: (y ^ 1, c, m) if c == 1 else None)
    shards = [pick(at.core, weight, joined(at, got, other, axis))]
    for bit in at.lows:
        if shared:
            more = []
            for shard in shards:
                low, high = halves(shard, axis)
                got = at.over(pick(at.side, low, high), bit)
                more.append(joined(at, got, at.hop(got, lambda y, c, m: (y ^ 1, c, m)), axis))
            shards = shards + more
        else:
            shards = shards + [at.over(shard, bit) for shard in shards]
    return shards


def reduce_grad(at, grads, axis, tokens=(None, None, None)):
    parts = list(grads)
    for bit in reversed(at.lows):
        count = len(parts) // 2
        sent = [after(at.over(part, bit), tokens[0]) for part in parts[count:]]
        parts = [(a.astype(f32) + b.astype(f32)).astype(bf16) for a, b in zip(parts[:count], sent)]
    low, high = halves(parts[0], axis)
    got = after(at.hop(pick(at.side, high, low), lambda y, c, m: (y ^ 1, c, m)), tokens[1])
    half = pick(at.side, low, high).astype(f32) + got.astype(f32)
    step = 2
    while step < at.rows:
        got = at.hop(half.astype(bf16), lambda y, c, m: (y ^ step, c, m))
        half = half + got.astype(f32)
        step = step * 2
    half = half.astype(bf16)
    moved = after(
        at.hop(half, lambda y, c, m: (y, c, m ^ at.top) if c == 1 else None), tokens[2]
    )
    half = pick(at.core, half, moved)
    first, second = halves(half, axis)
    got = at.other_core(pick(at.core, second, first))
    quarter = (pick(at.core, first, second).astype(f32) + got.astype(f32)).astype(bf16)
    across = at.hop(quarter, lambda y, c, m: (y ^ 1, c, m))
    mine = jnp.stack([pick(at.side, quarter, across), pick(at.side, across, quarter)])
    theirs = at.other_core(mine)
    even, odd = pick(at.core, mine, theirs), pick(at.core, theirs, mine)
    return jnp.concatenate([even[0], odd[0], even[1], odd[1]], axis=axis).astype(f32)


def gather_tokens(at, block):
    beyond = at.partner(block)
    return jnp.concatenate([block, at.other_core(block), beyond, at.other_core(beyond)], axis=0)


def scatter_tokens(at, part, size):
    width = part.shape[1]
    blocks = part.reshape(2, 2, size, width)
    got = at.other_core(blocks[:, 1])
    kept = blocks[:, 0].astype(f32) + got.astype(f32)
    beyond = at.partner(kept[1].astype(bf16))
    return kept[0] + beyond.astype(f32)


def ordered(at, value, size):
    blocks = value.reshape((2, 2, size) + value.shape[1:])
    turned = blocks[:, ::-1]
    return pick(at.core, blocks, turned).reshape((2, 2 * size) + value.shape[1:])


def unordered(at, value, size):
    blocks = value.reshape((2, 2, size) + value.shape[2:])
    turned = blocks[:, ::-1]
    return pick(at.core, blocks, turned).reshape((4 * size,) + value.shape[2:])


def head_lanes(h, base=0):
    return slice(base + h * head_size, base + (h + 1) * head_size)


head_size = 128


def seats(core_ref, size):
    return [pl.ds(pl.multiple_of((a ^ core_ref[0]) * size, size), size) for a in range(2)]


def decay_block(a, b, size, h, cum_ref, cum_row_ref, seg_ref, seg_row_ref):
    rows, cols = slice(a * size, (a + 1) * size), slice(b * size, (b + 1) * size)
    differ = cum_ref[0, rows, h : h + 1] - cum_row_ref[0, h : h + 1, cols]
    same = seg_ref[0, rows, :] == seg_row_ref[0, :, cols]
    if a == b:
        same = same & (
            lax.broadcasted_iota(jnp.int32, (size, size), 0)
            >= lax.broadcasted_iota(jnp.int32, (size, size), 1)
        )
    return jnp.where(same, jnp.exp(jnp.minimum(differ, 0.0)), 0.0)


def state_kernel(core_ref, qkv_ref, tail_ref, out_ref):
    size = qkv_ref.shape[0] // 2
    count = tail_ref.shape[2]
    spots = seats(core_ref, size)
    for h in range(count):
        total = jnp.zeros((head_size, head_size), f32)
        for a in range(2):
            key = qkv_ref[spots[a], head_lanes(h, count * head_size)]
            value = qkv_ref[spots[a], head_lanes(h, 2 * count * head_size)]
            tail = tail_ref[0, a * size : (a + 1) * size, h : h + 1]
            total = total + t_mm((key.astype(f32) * tail).astype(bf16), value)
        out_ref[0, h] = total


def forward_kernel(
    core_ref, qkv_ref, swish_ref, state_ref, entry_ref, cum_ref, cum_row_ref, seg_ref, seg_row_ref,
    gated_ref, out_ref,
):
    size = qkv_ref.shape[0] // 2
    count = cum_ref.shape[2]
    spots = seats(core_ref, size)
    for h in range(count):
        state = state_ref[0, h].astype(bf16)
        for a in range(2):
            query = qkv_ref[spots[a], head_lanes(h)]
            out = mm(query, state) * entry_ref[0, a * size : (a + 1) * size, h : h + 1]
            for b in range(a + 1):
                key = qkv_ref[spots[b], head_lanes(h, count * head_size)]
                value = qkv_ref[spots[b], head_lanes(h, 2 * count * head_size)]
                decay = decay_block(a, b, size, h, cum_ref, cum_row_ref, seg_ref, seg_row_ref)
                out = out + mm((mm_t(query, key) * decay).astype(bf16), value)
            out_ref[spots[a], head_lanes(h)] = out
            centered = out - jnp.mean(out, axis=-1, keepdims=True)
            inverse = lax.rsqrt(jnp.mean(centered * centered, axis=-1, keepdims=True) + group_eps)
            swish = swish_ref[spots[a], head_lanes(h)]
            gated = centered * inverse * (swish * jax.nn.sigmoid(swish))
            gated_ref[spots[a], head_lanes(h)] = gated.astype(bf16)


def norm_back_kernel(
    core_ref, grad_ref, out_ref, swish_ref, qkv_ref, entry_ref, swish_grad_ref, head_grad_ref, state_ref
):
    size = qkv_ref.shape[0] // 2
    count = entry_ref.shape[2]
    spots = seats(core_ref, size)
    for h in range(count):
        total = jnp.zeros((head_size, head_size), f32)
        for a in range(2):
            lanes = head_lanes(h)
            out = out_ref[spots[a], lanes]
            centered = out - jnp.mean(out, axis=-1, keepdims=True)
            inverse = lax.rsqrt(jnp.mean(centered * centered, axis=-1, keepdims=True) + group_eps)
            normed = centered * inverse
            swish = swish_ref[spots[a], lanes]
            grad = grad_ref[spots[a], lanes]
            logistic = jax.nn.sigmoid(swish)
            slope = logistic * (1.0 + swish * (1.0 - logistic))
            swish_grad_ref[spots[a], lanes] = (grad * normed * slope).astype(bf16)
            grouped = grad * (swish * logistic)
            head_grad = inverse * (
                grouped
                - jnp.mean(grouped, axis=-1, keepdims=True)
                - normed * jnp.mean(grouped * normed, axis=-1, keepdims=True)
            )
            low = head_grad.astype(bf16)
            head_grad_ref[spots[a], lanes] = low
            entry = entry_ref[0, a * size : (a + 1) * size, h : h + 1]
            query = qkv_ref[spots[a], lanes].astype(f32) * entry
            total = total + t_mm(query.astype(bf16), low)
        state_ref[0, h] = total


def back_kernel(
    core_ref, qkv_ref, head_grad_ref, state_ref, later_ref, entry_ref, tail_ref, cum_ref, cum_row_ref,
    seg_ref, seg_row_ref, low_ref, cum_grad_ref,
):
    size = qkv_ref.shape[0] // 2
    count = cum_ref.shape[2]
    spots = seats(core_ref, size)
    for h in range(count):
        state, later = state_ref[0, h].astype(bf16), later_ref[0, h].astype(bf16)
        query = [qkv_ref[spots[a], head_lanes(h)] for a in range(2)]
        key = [qkv_ref[spots[a], head_lanes(h, count * head_size)] for a in range(2)]
        value = [qkv_ref[spots[a], head_lanes(h, 2 * count * head_size)] for a in range(2)]
        grad = [head_grad_ref[spots[a], head_lanes(h)] for a in range(2)]
        grad_query, grad_key, grad_value = [], [], []
        for a in range(2):
            rows = slice(a * size, (a + 1) * size)
            entry, tail = entry_ref[0, rows, h : h + 1], tail_ref[0, rows, h : h + 1]
            grad_query.append(mm_t(grad[a], state) * entry)
            grad_key.append(mm_t(value[a], later) * tail)
            grad_value.append(mm(key[a], later) * tail)
        for a in range(2):
            for b in range(a + 1):
                decay = decay_block(a, b, size, h, cum_ref, cum_row_ref, seg_ref, seg_row_ref)
                scores = (mm_t(query[a], key[b]) * decay).astype(bf16)
                grad_scores = (mm_t(grad[a], value[b]) * decay).astype(bf16)
                grad_query[a] = grad_query[a] + mm(grad_scores, key[b])
                grad_key[b] = grad_key[b] + t_mm(grad_scores, query[a])
                grad_value[b] = grad_value[b] + t_mm(scores, grad[a])
        for a in range(2):
            low_ref[spots[a], head_lanes(h)] = grad_query[a].astype(bf16)
            low_ref[spots[a], head_lanes(h, count * head_size)] = grad_key[a].astype(bf16)
            low_ref[spots[a], head_lanes(h, 2 * count * head_size)] = grad_value[a].astype(bf16)
            both = query[a].astype(f32) * grad_query[a] - key[a].astype(f32) * grad_key[a]
            cum_grad_ref[0, a * size : (a + 1) * size, h : h + 1] = jnp.sum(
                both, axis=-1, keepdims=True
            )


def per_sequence(kernel, core, arrays, outs, cost):
    def spec(shape):
        if len(shape) == 2:
            return pl.BlockSpec((shape[0] // 2, shape[1]), lambda i, c: (i, 0))
        rest = tuple(shape[1:])
        return pl.BlockSpec((1,) + rest, lambda i, c: (i,) + (0,) * len(rest))

    return pl.pallas_call(
        kernel,
        grid_spec=pltpu.PrefetchScalarGridSpec(
            num_scalar_prefetch=1,
            grid=(2,),
            in_specs=[spec(x.shape) for x in arrays],
            out_specs=[spec(o.shape) for o in outs],
        ),
        out_shape=outs,
        cost_estimate=pl.CostEstimate(
            flops=cost, transcendentals=0, bytes_accessed=sum(x.size * x.dtype.itemsize for x in arrays)
        ),
        compiler_params=pltpu.CompilerParams(vmem_limit_bytes=48 * 1024 * 1024),
    )(core, *arrays)


def struct(shape, kind=f32):
    return jax.ShapeDtypeStruct(shape, kind)


def per_device(
    inputs,
    cotangent,
    segment_ids,
    mixer_gain,
    query_weight,
    key_weight,
    value_weight,
    swish_weight,
    decay_weight,
    decay_bias,
    output_weight,
    feed_gain,
    gate_weight,
    up_weight,
    down_weight,
):
    at = Place()
    tokens = inputs[0].astype(f32)
    size, width = tokens.shape
    heads = decay_bias.shape[0]
    local_heads = query_weight.shape[1] // head_size
    own_ranks = [at.rank ^ (at.core * at.top)]
    for bit in at.lows:
        own_ranks = own_ranks + [r ^ bit for r in own_ranks]

    small = jnp.concatenate(
        [decay_weight.T, mixer_gain[None], feed_gain[None]], axis=0
    )
    bit = 1
    while bit < at.ways:
        got = at.over(small, bit)
        upper = (at.rank >> (bit.bit_length() - 1)) & 1
        small = jnp.concatenate([pick(upper, small, got), pick(upper, got, small)], axis=1)
        bit = bit * 2
    gain_one = small[heads].astype(f32)[None]
    gain_two = small[heads + 1].astype(f32)[None]
    decay_rows = jnp.concatenate(
        [lax.dynamic_slice_in_dim(small, r * local_heads, local_heads, 0) for r in own_ranks], axis=0
    )
    bias_own = jnp.concatenate(
        [lax.dynamic_slice_in_dim(decay_bias, r * local_heads, local_heads, 0) for r in own_ranks]
    )

    pair_ids = jnp.concatenate([segment_ids, at.partner(segment_ids)], axis=0)
    other_ids = at.other_core(pair_ids)
    segments = jnp.concatenate(
        [pick(at.core, pair_ids, other_ids), pick(at.core, other_ids, pair_ids)], axis=1
    )
    last_ids = segments[:, -1:]
    previous = at.hop(last_ids, lambda y, c, m: (y + 1, c, m) if y + 1 < at.rows else None)

    wide = jnp.concatenate([query_weight, key_weight, value_weight], axis=1)
    weights = {
        "qkv": gather_weight(at, wide, 0, False),
        "swish": gather_weight(at, swish_weight, 0, True),
        "output": gather_weight(at, output_weight, 1, True),
        "gate": gather_weight(at, gate_weight, 0, True),
        "up": gather_weight(at, up_weight, 0, True),
        "down": gather_weight(at, down_weight, 1, True),
    }
    shards = range(len(own_ranks))
    lanes = local_heads * head_size

    tokens_all = gather_tokens(at, inputs[0])
    grad_out_all = gather_tokens(at, cotangent[0])
    scale_one = lax.rsqrt(jnp.mean(tokens * tokens, axis=-1, keepdims=True) + rms_eps)
    wide_all = tokens_all.astype(f32)
    scale_all = lax.rsqrt(jnp.mean(wide_all * wide_all, axis=-1, keepdims=True) + rms_eps)
    normed_all = (wide_all * scale_all * gain_one).astype(bf16)

    decay_pre = mm_t(normed_all, decay_rows) + bias_own
    decays = ordered(at, -jax.nn.softplus(-decay_pre) / 16.0, size)
    span = 2 * size
    cumulative = jnp.cumsum(decays, axis=1)
    total = cumulative[:, -1:]
    entry = jnp.exp(cumulative) * (segments == previous)[:, :, None].astype(f32)
    tail = jnp.exp(total - cumulative) * (segments == last_ids)[:, :, None].astype(f32)
    keep = jnp.exp(total[:, 0]) * (last_ids == previous).astype(f32)
    cum_rows = cumulative.transpose(0, 2, 1)
    core = at.core.reshape(1).astype(jnp.int32)
    seg_col, seg_row = segments[:, :, None], segments[:, None, :]
    states = struct((2, local_heads, head_size, head_size))
    unit = 2 * 2 * local_heads * head_size * size

    def retention_state(j, qkv):
        return per_sequence(
            state_kernel, core, [qkv, tail[..., heads_at(j)]], [states], 2 * unit * head_size
        )[0]

    def heads_at(j):
        return slice(j * local_heads, (j + 1) * local_heads)

    saved = []
    attn_part = None
    for j in shards:
        mine = heads_at(j)
        qkv = mm(normed_all, weights["qkv"][j]).astype(bf16)
        tail_state = retention_state(j, qkv)
        kept = keep[:, mine, None, None]
        incoming = jnp.zeros_like(tail_state)
        for _ in range(at.rows - 1):
            passed = (kept * incoming + tail_state).astype(bf16)
            incoming = at.hop(
                passed, lambda y, c, m: (y + 1, c, m) if y + 1 < at.rows else None
            ).astype(f32)
        swish_pre = mm(normed_all, weights["swish"][j])
        gated, outputs = per_sequence(
            forward_kernel,
            core,
            [qkv, swish_pre, incoming, entry[..., mine], cumulative[..., mine], cum_rows[:, mine], seg_col, seg_row],
            [struct((4 * size, lanes), bf16), struct((4 * size, lanes))],
            6 * unit * size,
        )
        part = mm(gated, weights["output"][j])
        attn_part = part if attn_part is None else attn_part + part
        saved.append((qkv, swish_pre, tail_state, incoming, outputs, gated))

    attended = scatter_tokens(at, attn_part.astype(bf16), size)
    mixed = tokens + attended
    scale_two = lax.rsqrt(jnp.mean(mixed * mixed, axis=-1, keepdims=True) + rms_eps)
    normed_two = (mixed * scale_two * gain_two).astype(bf16)
    two_all = gather_tokens(at, normed_two)

    down_part, two_part = 0.0, 0.0
    grads = {name: [] for name in weights}
    for j in shards:
        gate_pre = mm(two_all, weights["gate"][j])
        up_pre = mm(two_all, weights["up"][j])
        logistic = jax.nn.sigmoid(gate_pre)
        hidden = (gate_pre * logistic * up_pre).astype(bf16)
        down_part = down_part + mm(hidden, weights["down"][j])
        grad_hidden = mm_t(grad_out_all, weights["down"][j])
        grad_gate = (grad_hidden * up_pre * silu_slope(gate_pre)).astype(bf16)
        grad_up = (grad_hidden * gate_pre * logistic).astype(bf16)
        two_part = two_part + mm_t(grad_gate, weights["gate"][j]) + mm_t(grad_up, weights["up"][j])
        grads["down"].append(t_mm(hidden, grad_out_all).astype(bf16))
        grads["gate"].append(t_mm(two_all, grad_gate).astype(bf16))
        grads["up"].append(t_mm(two_all, grad_up).astype(bf16))
    grad_two = scatter_tokens(at, two_part.astype(bf16), size)
    base_two = mixed * scale_two
    feed_part = jnp.sum(grad_two * base_two, axis=0)
    scaled_two = grad_two * gain_two
    grad_mixed = cotangent[0].astype(f32) + scale_two * (
        scaled_two - base_two * jnp.mean(scaled_two * base_two, axis=-1, keepdims=True)
    )
    attended_all = gather_tokens(at, grad_mixed.astype(bf16))
    layer_out = (
        mixed + scatter_tokens(at, after(down_part.astype(bf16), grad_mixed), size)
    ).astype(bf16)[None]

    normed_part = 0.0
    grad_decays, marks = [], []
    for j in shards:
        mine = heads_at(j)
        qkv, swish_pre, tail_state, incoming, outputs, gated = saved[j]
        kept = keep[:, mine, None, None]
        grad_gated = mm_t(attended_all, weights["output"][j])
        grad_swish, grad_heads, own_grad = per_sequence(
            norm_back_kernel,
            core,
            [grad_gated, outputs, swish_pre, qkv, entry[..., mine]],
            [struct((4 * size, lanes), bf16), struct((4 * size, lanes), bf16), states],
            2 * unit * head_size,
        )
        grads["output"].append(t_mm(gated, attended_all).astype(bf16))
        later = jnp.zeros_like(own_grad)
        for _ in range(at.rows - 1):
            passed = (kept * later + own_grad).astype(bf16)
            later = at.hop(
                passed, lambda y, c, m: (y - 1, c, m) if y > 0 else None
            ).astype(f32)
        normed_part = normed_part + mm_t(grad_swish, weights["swish"][j])
        grads["swish"].append(t_mm(normed_all, grad_swish).astype(bf16))
        crossing = jnp.sum(later * (kept * incoming + tail_state), axis=(-2, -1))
        lows, grad_cum = per_sequence(
            back_kernel,
            core,
            [qkv, grad_heads, incoming, later, entry[..., mine], tail[..., mine], cumulative[..., mine], cum_rows[:, mine], seg_col, seg_row],
            [struct((4 * size, 3 * lanes), bf16), struct((2, span, local_heads))],
            15 * unit * size,
        )
        grad_decays.append(
            jnp.cumsum(grad_cum[:, ::-1], axis=1)[:, ::-1] + crossing[:, None]
        )
        normed_part = normed_part + mm_t(lows, weights["qkv"][j])
        grads["qkv"].append(t_mm(normed_all, lows).astype(bf16))
        marks.append((grad_heads, lows))
    grad_decay = unordered(at, jnp.concatenate(grad_decays, axis=-1), size)
    decay_pre_grad = grad_decay * jax.nn.sigmoid(-decay_pre) / 16.0
    decay_low = decay_pre_grad.astype(bf16)
    normed_part = normed_part + mm(decay_low, decay_rows)
    decay_part = t_mm(decay_low, normed_all)
    bias_part = jnp.sum(decay_pre_grad, axis=0)

    grad_normed = scatter_tokens(at, normed_part.astype(bf16), size)
    base_one = tokens * scale_one
    mixer_part = jnp.sum(grad_normed * base_one, axis=0)
    scaled_one = grad_normed * gain_one
    input_grad = (
        grad_mixed
        + scale_one
        * (scaled_one - base_one * jnp.mean(scaled_one * base_one, axis=-1, keepdims=True))
    ).astype(bf16)[None]

    pad_rows = jnp.zeros((heads, width), f32)
    pad_bias = jnp.zeros((heads,), f32)
    for i, r in enumerate(own_ranks):
        rows = slice(i * local_heads, (i + 1) * local_heads)
        pad_rows = lax.dynamic_update_slice_in_dim(pad_rows, decay_part[rows], r * local_heads, 0)
        pad_bias = lax.dynamic_update_slice_in_dim(pad_bias, bias_part[rows], r * local_heads, 0)
    piece = width // at.ways
    bias_row = jnp.tile(jnp.pad(pad_bias, (0, piece - heads)), at.ways)
    sums = jnp.concatenate(
        [pad_rows, mixer_part[None], feed_part[None], bias_row[None]], axis=0
    )
    bit = at.top
    while bit > 0:
        low, high = halves(sums, 1)
        upper = (at.rank >> (bit.bit_length() - 1)) & 1
        sums = pick(upper, low, high) + at.over(pick(upper, high, low), bit)
        bit = bit // 2
    sums = sums + at.other_core(sums)
    step = 1
    while step < at.rows:
        sums = sums + at.hop(sums, lambda y, c, m: (y ^ step, c, m))
        step = step * 2

    first, last = marks[0], marks[-1]
    total_of = {}
    for name in ("down", "gate", "up"):
        total_of[name] = reduce_grad(
            at, grads[name], 1 if name == "down" else 0, (attended_all, first[1], last[1])
        )
    total_of["output"] = reduce_grad(at, grads["output"], 1, (last[1], None, None))
    total_of["swish"] = reduce_grad(at, grads["swish"], 0, (last[1], None, None))
    wide_total = reduce_grad(at, grads["qkv"], 0)
    return (
        layer_out,
        input_grad,
        sums[heads],
        wide_total[:, :lanes],
        wide_total[:, lanes : 2 * lanes],
        wide_total[:, 2 * lanes :],
        total_of["swish"],
        sums[:heads].T,
        sums[heads + 2][:heads],
        total_of["output"],
        sums[heads + 1],
        total_of["gate"],
        total_of["up"],
        total_of["down"],
    )


def solution(mesh):
    placed = (
        P("mp", "seq", None),
        P("mp", "seq", None),
        P("mp", "seq"),
        P("mp"),
        P(None, "mp"),
        P(None, "mp"),
        P(None, "mp"),
        P(None, "mp"),
        P("mp", None),
        P(),
        P("mp", None),
        P("mp"),
        P(None, "mp"),
        P(None, "mp"),
        P("mp", None),
    )
    return jax.shard_map(
        per_device,
        mesh=mesh,
        in_specs=placed,
        out_specs=(
            P("mp", "seq", None),
            P("mp", "seq", None),
            P("mp"),
            P(None, "mp"),
            P(None, "mp"),
            P(None, "mp"),
            P(None, "mp"),
            P("mp", None),
            P(),
            P("mp", None),
            P("mp"),
            P(None, "mp"),
            P(None, "mp"),
            P("mp", None),
        ),
        check_vma=False,
    )
```

time: 1730 us -> 1080 us (0.62)
  waiting for transfers between devices: 1130 us -> 562 us
  blocking collectives: 120 us -> 0 us
  starting transfers between devices: 8.16 us -> 125 us
  matrix products: 302 us -> 211 us
  Pallas kernels: 0 us -> 31.3 us
    reduce_scatter x5 -> x0, waiting for transfers between devices: 581 us -> none  [the longest x1 148 us: tensor_body(): lax.psum_scatter(two_part.reshape(groups, length_rows, width).astype(jnp....]
    ppermute x1 -> x94, waiting for transfers between devices: 0.01 us -> 562 us  [hop(): return lax.ppermute(value, ('seq', 'mp'), pairs)]
    all_gather x6 -> x0, waiting for transfers between devices: 395 us -> none  [the longest x1 123 us: tensor_body(): lax.all_gather(normed_two[None], 'mp', axis=0, tiled=True)]
    psum x1 -> x0, waiting for transfers between devices: 150 us -> none  [tensor_body(): lax.psum(query_local.astype(jnp.bfloat16), 'seq').astype(jnp.float32)]
    ppermute x1 -> x94, starting transfers between devices: 7.46 us -> 125 us  [hop(): return lax.ppermute(value, ('seq', 'mp'), pairs)]
    dot_general x39, matrix products: 302 us -> 211 us  [dot(): lax.dot_general(left, right, ((dims[0], dims[1]), ((), ())), preferred_el...]
    all_gather x5 -> x0, blocking collectives: 76.7 us -> none  [the longest x1 24.8 us: tensor_body(): lax.all_gather(decay_weight, 'mp', axis=0, tiled=True)]
    unnamed x2 -> x0, blocking collectives: 34.7 us -> none
  transfers between devices with their start and end apart: 13 -> 94, of which waited for: 10 -> 43; matrix products, arithmetic and copies ran while one was open for 13% -> 25% of each run, Pallas kernels for 0% -> 3%
where the time goes in v1:
time: 1080 us
  waiting for transfers between devices  562 us (52%)
  matrix products  211 us (20%)
  starting transfers between devices  125 us (12%)
  other arithmetic  97.9 us (9%)
  local copies, waits for them, and re-layouts  45.1 us (4%)
  Pallas kernels  31.3 us (3%)
    ppermute x94, waiting for transfers between devices, hop(): return lax.ppermute(value, ('seq', 'mp'), pairs)  562 us
    dot_general x39, matrix products, dot(): lax.dot_general(left, right, ((dims[0], dims[1]), ((), ())), preferred_el...  211 us
    ppermute x94, starting transfers between devices, hop(): return lax.ppermute(value, ('seq', 'mp'), pairs)  125 us
    select_n x61, other arithmetic, pick(): return jnp.where(flag == 0, first, second)  43.8 us
    pallas_call x8, Pallas kernels, per_sequence(): pl.pallas_call(kernel, grid_spec=pltpu.PrefetchScalarGridSpec(num_scalar_...  31.3 us
  transfers between devices with their start and end apart: 94, of which 43 were waited for; matrix products, arithmetic and copies ran while one was open for 25% of the time, Pallas kernels for 3%

profile of v1, /device:TPU:1, one launch (start us, length us, event | category | flops | bytes accessed | tf_op | source)
XLA Modules:
  0.0 1076.4 jit_solution(3355129656567686078)
XLA Ops:
  25.2 17.9 %collective-permute-done.10 = s32[1,256]{1,0:T(1,128)S(1)} collective-permute-done((s32[1,256]{1,0:T(1,128)S(1)}, s32[1,256]{1,0:T(1,128)S(1)}, u32[]{:S(2)}, u32[]{:S(2)}) %collective-permute-start.10) | collective-permute-done | bytes 1056 | tf_op jit(solution)/shard_map/ppermute | solution.py:55
  53.3 6.6 collective-permute-done.4
  72.9 10.1 collective-permute-done.14
  119.9 28.2 %collective-permute-done.27 = bf16[1024,688]{0,1:T(8,128)(2,1)} collective-permute-done((bf16[1024,688]{0,1:T(8,128)(2,1)}, bf16[1024,688]{0,1:T(8,128)(2,1)}, u32[]{:S(2)}, u32[]{:S(2)}) %collective-permute-start.27) | collective-permute-done | bytes 1409056 | tf_op jit(solution)/shard_map/ppermute | solution.py:55
  151.2 12.0 %collective-permute-done.29 = bf16[1024,688]{0,1:T(8,128)(2,1)} collective-permute-done((bf16[1024,688]{0,1:T(8,128)(2,1)}, bf16[1024,688]{0,1:T(8,128)(2,1)}, u32[]{:S(2)}, u32[]{:S(2)}) %collective-permute-start.29) | collective-permute-done | bytes 1409056 | tf_op jit(solution)/shard_map/ppermute | solution.py:55
  166.9 11.5 %collective-permute-done.31 = bf16[688,1024]{1,0:T(8,128)(2,1)} collective-permute-done((bf16[688,1024]{1,0:T(8,128)(2,1)}, bf16[688,1024]{1,0:T(8,128)(2,1)}, u32[]{:S(2)}, u32[]{:S(2)}) %collective-permute-start.31) | collective-permute-done | bytes 1409056 | tf_op jit(solution)/shard_map/ppermute | solution.py:55
  203.6 16.4 %collective-permute-done.21 = bf16[256,1024]{1,0:T(8,128)(2,1)} collective-permute-done((bf16[256,1024]{1,0:T(8,128)(2,1)}, bf16[256,1024]{1,0:T(8,128)(2,1)}, u32[]{:S(2)}, u32[]{:S(2)}) %collective-permute-start.21) | collective-permute-done | bytes 524320 | tf_op jit(solution)/shard_map/ppermute | solution.py:55
  221.3 6.9 convolution_convert_fusion.13.qkv_ref
  281.0 21.0 %collective-permute-done.33 = bf16[1024,688]{0,1:T(8,128)(2,1)} collective-permute-done((bf16[1024,688]{0,1:T(8,128)(2,1)}, bf16[1024,688]{0,1:T(8,128)(2,1)}, u32[]{:S(2)}, u32[]{:S(2)}) %collective-permute-start.33) | collective-permute-done | bytes 1409056 | tf_op jit(solution)/shard_map/ppermute | solution.py:55
  303.1 29.1 %collective-permute-done.35 = bf16[1024,688]{0,1:T(8,128)(2,1)} collective-permute-done((bf16[1024,688]{0,1:T(8,128)(2,1)}, bf16[1024,688]{0,1:T(8,128)(2,1)}, u32[]{:S(2)}, u32[]{:S(2)}) %collective-permute-start.35) | collective-permute-done | bytes 1409056 | tf_op jit(solution)/shard_map/ppermute | solution.py:55
  332.1 29.8 %collective-permute-done.37 = bf16[688,1024]{1,0:T(8,128)(2,1)S(1)} collective-permute-done((bf16[688,1024]{1,0:T(8,128)(2,1)S(1)}, bf16[688,1024]{1,0:T(8,128)(2,1)S(1)}, u32[]{:S(2)}, u32[]{:S(2)}) %collective-permute-start.37) | collective-permute-done | bytes 1409056 | tf_op jit(solution)/shard_map/ppermute | solution.py:55
  367.5 27.9 %collective-permute-done.38 = bf16[688,1024]{1,0:T(8,128)(2,1)S(1)} collective-permute-done((bf16[688,1024]{1,0:T(8,128)(2,1)S(1)}, bf16[688,1024]{1,0:T(8,128)(2,1)S(1)}, u32[]{:S(2)}, u32[]{:S(2)}) %collective-permute-start.38) | collective-permute-done | bytes 1409056 | tf_op jit(solution)/shard_map/ppermute | solution.py:55
  399.3 6.4 fusion.30
  410.6 9.5 multiply_convert_fusion
  420.1 8.7 fusion.29
  432.0 7.0 fusion.66
  439.0 7.7 multiply_convert_fusion.2
  452.5 6.2 fusion.83
  458.7 15.2 %add_convert_fusion.1 = bf16[1024,2048]{1,0:T(8,128)(2,1)} fusion(f32[1024,2048]{1,0:T(8,128)} %fusion.29, f32[1024,2048]{1,0:T(8,128)} %fusion.82, f32[1024,2048]{1,0:T(8,128)} %fusion.83, bf16[1024,688]{0,1:T(8,128)(2,1)} %get-tuple-element.79, bf16[1024,688]{0,1:T(8,128)(2,1)} %copy-done.72, bf16[1024,688]{0,1:T(8,128)(2,1)S(1)} %get-tuple-element.103), kind=kOutput, calls=%fused_computation.6 | convolution fusion | flops 2899705856 | bytes 33587200 | tf_op jit(solution)/shard_map/dot_general | solution.py:15
  477.0 6.3 convolution_convert_fusion.4
  490.7 6.8 add_convert_fusion.2
  497.5 12.9 %collective-permute-done.43 = bf16[256,2048]{1,0:T(8,128)(2,1)S(1)} collective-permute-done((bf16[256,2048]{1,0:T(8,128)(2,1)}, bf16[256,2048]{1,0:T(8,128)(2,1)S(1)}, u32[]{:S(2)}, u32[]{:S(2)}) %collective-permute-start.43) | collective-permute-done | bytes 1048608 | tf_op jit(solution)/shard_map/ppermute | solution.py:55
  522.4 6.5 convolution_convert_fusion.6
  529.1 16.8 %collective-permute-done.47 = bf16[256,2048]{1,0:T(8,128)(2,1)S(1)} collective-permute-done((bf16[256,2048]{1,0:T(8,128)(2,1)S(1)}, bf16[256,2048]{1,0:T(8,128)(2,1)S(1)}, u32[]{:S(2)}, u32[]{:S(2)}) %collective-permute-start.47) | collective-permute-done | bytes 1048608 | tf_op jit(solution)/shard_map/ppermute | solution.py:55
  567.7 5.9 add_convert_fusion.7
  576.0 36.9 %collective-permute-done.82 = bf16[2048,688]{0,1:T(8,128)(2,1)} collective-permute-done((bf16[2048,688]{0,1:T(8,128)(2,1)}, bf16[2048,688]{0,1:T(8,128)(2,1)}, u32[]{:S(2)}, u32[]{:S(2)}) %collective-permute-start.82) | collective-permute-done | bytes 2818080 | tf_op jit(solution)/shard_map/ppermute | solution.py:55
  628.8 44.5 %collective-permute-done.88 = bf16[688,2048]{1,0:T(8,128)(2,1)} collective-permute-done((bf16[688,2048]{1,0:T(8,128)(2,1)}, bf16[688,2048]{1,0:T(8,128)(2,1)}, u32[]{:S(2)}, u32[]{:S(2)}) %collective-permute-start.88) | collective-permute-done | bytes 2818080 | tf_op jit(solution)/shard_map/ppermute | solution.py:55
  674.5 5.8 add_convert_fusion.5
  682.5 6.2 shard_map.261
  700.2 6.2 shard_map.259
  719.8 7.5 fusion.86
  737.7 7.7 fusion.87
  745.4 14.3 %add_convert_fusion = bf16[1024,2048]{1,0:T(8,128)(2,1)} fusion(f32[1024,2048]{1,0:T(8,128)} %fusion.47, f32[1024,2048]{1,0:T(8,128)} %fusion.87, f32[1024,2048]{1,0:T(8,128)} %fusion.85, f32[1024,2048]{1,0:T(8,128)} %fusion.86, bf16[1024,256]{1,0:T(8,128)(2,1)S(1)} %copy-done.21, bf16[1024,256]{1,0:T(8,128)(2,1)S(1)} %copy-done.88, ...), kind=kOutput, calls=%fused_computation.5 | convolution fusion | flops 1086324736 | bytes 39321600 | tf_op jit(solution)/shard_map/dot_general | solution.py:15
  777.7 14.4 %collective-permute-done.89 = bf16[688,1024]{1,0:T(8,128)(2,1)S(1)} collective-permute-done((bf16[688,1024]{1,0:T(8,128)(2,1)S(1)}, bf16[688,1024]{1,0:T(8,128)(2,1)S(1)}, u32[]{:S(2)}, u32[]{:S(2)}) %collective-permute-start.89) | collective-permute-done | bytes 1409056 | tf_op jit(solution)/shard_map/ppermute | solution.py:55
  796.7 6.5 collective-permute-done.65
  805.9 8.6 collective-permute-done.71
  818.4 25.5 %collective-permute-done.66 = bf16[1024,256]{1,0:T(8,128)(2,1)S(1)} collective-permute-done((bf16[1024,256]{1,0:T(8,128)(2,1)S(1)}, bf16[1024,256]{1,0:T(8,128)(2,1)S(1)}, u32[]{:S(2)}, u32[]{:S(2)}) %collective-permute-start.66) | collective-permute-done | bytes 524320 | tf_op jit(solution)/shard_map/ppermute | solution.py:55
  845.9 18.7 %collective-permute-done.72 = bf16[256,1024]{1,0:T(8,128)(2,1)S(1)} collective-permute-done((bf16[256,1024]{1,0:T(8,128)(2,1)S(1)}, bf16[256,1024]{1,0:T(8,128)(2,1)S(1)}, u32[]{:S(2)}, u32[]{:S(2)}) %collective-permute-start.72) | collective-permute-done | bytes 524320 | tf_op jit(solution)/shard_map/ppermute | solution.py:55
  875.1 5.9 collective-permute-done.74
  883.0 11.9 %collective-permute-done.84 = bf16[1024,688]{0,1:T(8,128)(2,1)S(1)} collective-permute-done((bf16[1024,688]{0,1:T(8,128)(2,1)S(1)}, bf16[1024,688]{0,1:T(8,128)(2,1)S(1)}, u32[]{:S(2)}, u32[]{:S(2)}) %collective-permute-start.84) | collective-permute-done | bytes 1409056 | tf_op jit(solution)/shard_map/ppermute | solution.py:55
  895.3 14.7 %collective-permute-done.90 = bf16[688,1024]{1,0:T(8,128)(2,1)S(1)} collective-permute-done((bf16[688,1024]{1,0:T(8,128)(2,1)S(1)}, bf16[688,1024]{1,0:T(8,128)(2,1)S(1)}, u32[]{:S(2)}, u32[]{:S(2)}) %collective-permute-start.90) | collective-permute-done | bytes 1409056 | tf_op jit(solution)/shard_map/ppermute | solution.py:55
  912.8 13.6 %collective-permute-done.52 = bf16[256,2048]{1,0:T(8,128)(2,1)S(1)} collective-permute-done((bf16[256,2048]{1,0:T(8,128)(2,1)S(1)}, bf16[256,2048]{1,0:T(8,128)(2,1)S(1)}, u32[]{:S(2)}, u32[]{:S(2)}) %collective-permute-start.52) | collective-permute-done | bytes 1048608 | tf_op jit(solution)/shard_map/ppermute | solution.py:55
  948.1 32.8 %collective-permute-done.57 = f32[19,256]{1,0:T(8,128)S(1)} collective-permute-done((f32[19,256]{1,0:T(8,128)S(1)}, f32[19,256]{1,0:T(8,128)S(1)}, u32[]{:S(2)}, u32[]{:S(2)}) %collective-permute-start.57) | collective-permute-done | bytes 19488 | tf_op jit(solution)/shard_map/ppermute | solution.py:55
  985.2 12.5 %collective-permute-done.80 = bf16[512,688]{0,1:T(8,128)(2,1)S(1)} collective-permute-done((bf16[512,688]{0,1:T(8,128)(2,1)S(1)}, bf16[512,688]{0,1:T(8,128)(2,1)S(1)}, u32[]{:S(2)}, u32[]{:S(2)}) %collective-permute-start.80) | collective-permute-done | bytes 704544 | tf_op jit(solution)/shard_map/ppermute | solution.py:55
  1005.3 7.5 collective-permute-done.86
  1016.3 11.6 %collective-permute-done.92 = bf16[688,512]{1,0:T(8,128)(2,1)S(1)} collective-permute-done((bf16[688,512]{1,0:T(8,128)(2,1)S(1)}, bf16[688,512]{1,0:T(8,128)(2,1)S(1)}, u32[]{:S(2)}, u32[]{:S(2)}) %collective-permute-start.92) | collective-permute-done | bytes 704544 | tf_op jit(solution)/shard_map/ppermute | solution.py:55
  1030.1 10.0 collective-permute-done.60
  1044.7 17.4 %collective-permute-done.62 = bf16[512,768]{1,0:T(8,128)(2,1)S(1)} collective-permute-done((bf16[512,768]{1,0:T(8,128)(2,1)S(1)}, bf16[512,768]{1,0:T(8,128)(2,1)S(1)}, u32[]{:S(2)}, u32[]{:S(2)}) %collective-permute-start.62) | collective-permute-done | bytes 786464 | tf_op jit(solution)/shard_map/ppermute | solution.py:55
  (720 shorter events, 398.3 us)
Async XLA Ops:
  0.6 84.3 %collective-permute-start.1 = (bf16[256,2048]{1,0:T(8,128)(2,1)}, bf16[256,2048]{1,0:T(8,128)(2,1)}, u32[]{:S(2)}, u32[]{:S(2)}) collective-permute-start(bf16[256,2048]{1,0:T(8,128)(2,1)} %bitcast.277), channel_id=1, source_target_pairs={{0,2},{1,3},{2,0},{3,1},{4,6},{5,7},{6,4},{7,5},{8,10},{9,11},{10,... | collective-permute-start | bytes 3145736 | tf_op jit(solution)/shard_map/ppermute | solution.py:55
  2.8 99.0 %collective-permute-start = (bf16[256,2048]{1,0:T(8,128)(2,1)}, bf16[256,2048]{1,0:T(8,128)(2,1)}, u32[]{:S(2)}, u32[]{:S(2)}) collective-permute-start(bf16[256,2048]{1,0:T(8,128)(2,1)} %bitcast.278), channel_id=1, source_target_pairs={{0,8},{1,9},{2,10},{3,11},{4,12},{5,13},{6,14},{7,15},{8,0},{9,1},... | collective-permute-start | bytes 3145736 | tf_op jit(solution)/shard_map/ppermute | solution.py:55
  5.8 47.3 %collective-permute-start.3 = (bf16[18,256]{1,0:T(8,128)(2,1)S(1)}, bf16[18,256]{1,0:T(8,128)(2,1)S(1)}, u32[]{:S(2)}, u32[]{:S(2)}) collective-permute-start(bf16[18,256]{1,0:T(8,128)(2,1)S(1)} %pad_maximum_fusion.32), channel_id=1, source_target_pairs={{0,1},{1,0},{2,3},{3,2},{4,5},{5,4},{6,7},{7,6},{8,9},{9,8},{10,11... | collective-permute-start | bytes 27656 | tf_op jit(solution)/shard_map/ppermute | solution.py:55
  11.4 92.3 %collective-permute-start.6 = (bf16[1024,768]{1,0:T(8,128)(2,1)}, bf16[1024,768]{1,0:T(8,128)(2,1)}, u32[]{:S(2)}, u32[]{:S(2)}) collective-permute-start(bf16[1024,768]{1,0:T(8,128)(2,1)} %slice_select_fusion), channel_id=1, source_target_pairs={{8,12},{9,13},{10,14},{11,15},{12,8},{13,9},{14,10},{15,11},{24,28... | collective-permute-start | bytes 4718600 | tf_op jit(solution)/shard_map/ppermute | solution.py:55
  83.1 65.1 %collective-permute-start.27 = (bf16[1024,688]{0,1:T(8,128)(2,1)}, bf16[1024,688]{0,1:T(8,128)(2,1)}, u32[]{:S(2)}, u32[]{:S(2)}) collective-permute-start(bf16[1024,688]{0,1:T(8,128)(2,1)} %slice_select_fusion.6), channel_id=1, source_target_pairs={{8,12},{9,13},{10,14},{11,15},{12,8},{13,9},{14,10},{15,11},{24,28... | collective-permute-start | bytes 4227080 | tf_op jit(solution)/shard_map/ppermute | solution.py:55
  95.2 68.0 %collective-permute-start.29 = (bf16[1024,688]{0,1:T(8,128)(2,1)}, bf16[1024,688]{0,1:T(8,128)(2,1)}, u32[]{:S(2)}, u32[]{:S(2)}) collective-permute-start(bf16[1024,688]{0,1:T(8,128)(2,1)} %slice_select_fusion.5), channel_id=1, source_target_pairs={{8,12},{9,13},{10,14},{11,15},{12,8},{13,9},{14,10},{15,11},{24,28... | collective-permute-start | bytes 4227080 | tf_op jit(solution)/shard_map/ppermute | solution.py:55
  101.8 76.6 %collective-permute-start.31 = (bf16[688,1024]{1,0:T(8,128)(2,1)}, bf16[688,1024]{1,0:T(8,128)(2,1)}, u32[]{:S(2)}, u32[]{:S(2)}) collective-permute-start(bf16[688,1024]{1,0:T(8,128)(2,1)} %slice_select_fusion.4), channel_id=1, source_target_pairs={{8,12},{9,13},{10,14},{11,15},{12,8},{13,9},{14,10},{15,11},{24,28... | collective-permute-start | bytes 4227080 | tf_op jit(solution)/shard_map/ppermute | solution.py:55
  103.7 45.7 %collective-permute-start.17 = (bf16[1024,256]{1,0:T(8,128)(2,1)}, bf16[1024,256]{1,0:T(8,128)(2,1)S(1)}, u32[]{:S(2)}, u32[]{:S(2)}) collective-permute-start(bf16[1024,256]{1,0:T(8,128)(2,1)} %slice_select_fusion.8), channel_id=1, source_target_pairs={{0,1},{1,0},{2,3},{3,2},{4,5},{5,4},{6,7},{7,6},{8,9},{9,8},{10,11... | collective-permute-start | bytes 1572872 | tf_op jit(solution)/shard_map/ppermute | solution.py:55
  105.0 86.6 %collective-permute-start.7 = (bf16[1024,768]{1,0:T(8,128)(2,1)}, bf16[1024,768]{1,0:T(8,128)(2,1)}, u32[]{:S(2)}, u32[]{:S(2)}) collective-permute-start(bf16[1024,768]{1,0:T(8,128)(2,1)} %collective-permute-done.6), channel_id=1, source_target_pairs={{8,24},{9,25},{10,26},{11,27},{12,28},{13,29},{14,30},{15,31},{24,... | collective-permute-start | bytes 4718600 | tf_op jit(solution)/shard_map/ppermute | solution.py:55
  163.3 70.0 %collective-permute-start.28 = (bf16[1024,688]{0,1:T(8,128)(2,1)}, bf16[1024,688]{0,1:T(8,128)(2,1)}, u32[]{:S(2)}, u32[]{:S(2)}) collective-permute-start(bf16[1024,688]{0,1:T(8,128)(2,1)} %collective-permute-done.27), channel_id=1, source_target_pairs={{8,24},{9,25},{10,26},{11,27},{12,28},{13,29},{14,30},{15,31},{24,... | collective-permute-start | bytes 4227080 | tf_op jit(solution)/shard_map/ppermute | solution.py:55
  178.4 91.7 %collective-permute-start.30 = (bf16[1024,688]{0,1:T(8,128)(2,1)}, bf16[1024,688]{0,1:T(8,128)(2,1)}, u32[]{:S(2)}, u32[]{:S(2)}) collective-permute-start(bf16[1024,688]{0,1:T(8,128)(2,1)} %collective-permute-done.29), channel_id=1, source_target_pairs={{8,24},{9,25},{10,26},{11,27},{12,28},{13,29},{14,30},{15,31},{24,... | collective-permute-start | bytes 4227080 | tf_op jit(solution)/shard_map/ppermute | solution.py:55
  182.0 94.2 %collective-permute-start.32 = (bf16[688,1024]{1,0:T(8,128)(2,1)}, bf16[688,1024]{1,0:T(8,128)(2,1)}, u32[]{:S(2)}, u32[]{:S(2)}) collective-permute-start(bf16[688,1024]{1,0:T(8,128)(2,1)} %collective-permute-done.31), channel_id=1, source_target_pairs={{8,24},{9,25},{10,26},{11,27},{12,28},{13,29},{14,30},{15,31},{24,... | collective-permute-start | bytes 4227080 | tf_op jit(solution)/shard_map/ppermute | solution.py:55
  184.1 35.8 %collective-permute-start.21 = (bf16[256,1024]{1,0:T(8,128)(2,1)}, bf16[256,1024]{1,0:T(8,128)(2,1)}, u32[]{:S(2)}, u32[]{:S(2)}) collective-permute-start(bf16[256,1024]{1,0:T(8,128)(2,1)} %collective-permute-done.20), channel_id=1, source_target_pairs={{0,16},{1,17},{2,18},{3,19},{4,20},{5,21},{6,22},{7,23},{8,24},{9,... | collective-permute-start | bytes 1572872 | tf_op jit(solution)/shard_map/ppermute | solution.py:55
  197.0 44.2 %collective-permute-start.16 = (bf16[2048,768]{1,0:T(8,128)(2,1)}, bf16[2048,768]{1,0:T(8,128)(2,1)}, u32[]{:S(2)}, u32[]{:S(2)}) collective-permute-start(bf16[2048,768]{1,0:T(8,128)(2,1)} %maximum_select_fusion), channel_id=1, source_target_pairs={{0,1},{1,0},{2,3},{3,2},{4,5},{5,4},{6,7},{7,6},{8,9},{9,8},{10,11... | collective-permute-start | bytes 9437192 | tf_op jit(solution)/shard_map/ppermute | solution.py:55
  274.5 57.6 %collective-permute-start.35 = (bf16[1024,688]{0,1:T(8,128)(2,1)}, bf16[1024,688]{0,1:T(8,128)(2,1)}, u32[]{:S(2)}, u32[]{:S(2)}) collective-permute-start(bf16[1024,688]{0,1:T(8,128)(2,1)} %slice_select_fusion.2), channel_id=1, source_target_pairs={{0,1},{1,0},{2,3},{3,2},{4,5},{5,4},{6,7},{7,6},{8,9},{9,8},{10,11... | collective-permute-start | bytes 4227080 | tf_op jit(solution)/shard_map/ppermute | solution.py:55
  280.2 81.7 %collective-permute-start.37 = (bf16[688,1024]{1,0:T(8,128)(2,1)S(1)}, bf16[688,1024]{1,0:T(8,128)(2,1)S(1)}, u32[]{:S(2)}, u32[]{:S(2)}) collective-permute-start(bf16[688,1024]{1,0:T(8,128)(2,1)S(1)} %slice_select_fusion.1), channel_id=1, source_target_pairs={{0,1},{1,0},{2,3},{3,2},{4,5},{5,4},{6,7},{7,6},{8,9},{9,8},{10,11... | collective-permute-start | bytes 4227080 | tf_op jit(solution)/shard_map/ppermute | solution.py:55
  302.0 59.9 %collective-permute-start.34 = (bf16[1024,688]{0,1:T(8,128)(2,1)}, bf16[1024,688]{0,1:T(8,128)(2,1)S(1)}, u32[]{:S(2)}, u32[]{:S(2)}) collective-permute-start(bf16[1024,688]{0,1:T(8,128)(2,1)} %collective-permute-done.33), channel_id=1, source_target_pairs={{0,16},{1,17},{2,18},{3,19},{4,20},{5,21},{6,22},{7,23},{8,24},{9,... | collective-permute-start | bytes 4227080 | tf_op jit(solution)/shard_map/ppermute | solution.py:55
  303.0 58.9 %collective-permute-start.25 = (bf16[256,2048]{1,0:T(8,128)(2,1)S(1)}, bf16[256,2048]{1,0:T(8,128)(2,1)S(1)}, u32[]{:S(2)}, u32[]{:S(2)}) collective-permute-start(bf16[256,2048]{1,0:T(8,128)(2,1)S(1)} %multiply_convert_fusion.6), channel_id=1, source_target_pairs={{0,2},{1,3},{2,0},{3,1},{4,6},{5,7},{6,4},{7,5},{8,10},{9,11},{10,... | collective-permute-start | bytes 3145736 | tf_op jit(solution)/shard_map/ppermute | solution.py:55
  361.9 35.3 %collective-permute-start.24 = (bf16[256,2048]{1,0:T(8,128)(2,1)S(1)}, bf16[256,2048]{1,0:T(8,128)(2,1)S(1)}, u32[]{:S(2)}, u32[]{:S(2)}) collective-permute-start(bf16[256,2048]{1,0:T(8,128)(2,1)S(1)} %multiply_convert_fusion.6), channel_id=1, source_target_pairs={{0,8},{1,9},{2,10},{3,11},{4,12},{5,13},{6,14},{7,15},{8,0},{9,1},... | collective-permute-start | bytes 3145736 | tf_op jit(solution)/shard_map/ppermute | solution.py:55
  361.9 35.3 %collective-permute-start.26 = (bf16[256,2048]{1,0:T(8,128)(2,1)S(1)}, bf16[256,2048]{1,0:T(8,128)(2,1)S(1)}, u32[]{:S(2)}, u32[]{:S(2)}) collective-permute-start(bf16[256,2048]{1,0:T(8,128)(2,1)S(1)} %collective-permute-done.25), channel_id=1, source_target_pairs={{0,8},{1,9},{2,10},{3,11},{4,12},{5,13},{6,14},{7,15},{8,0},{9,1},... | collective-permute-start | bytes 3145736 | tf_op jit(solution)/shard_map/ppermute | solution.py:55
  364.2 46.5 %collective-permute-start.39 = (bf16[256,2048]{1,0:T(8,128)(2,1)S(1)}, bf16[256,2048]{1,0:T(8,128)(2,1)}, u32[]{:S(2)}, u32[]{:S(2)}) collective-permute-start(bf16[256,2048]{1,0:T(8,128)(2,1)S(1)} %bitcast.292), channel_id=1, source_target_pairs={{0,8},{1,9},{2,10},{3,11},{4,12},{5,13},{6,14},{7,15},{8,0},{9,1},... | collective-permute-start | bytes 3145736 | tf_op jit(solution)/shard_map/ppermute | solution.py:55
  365.3 45.4 %collective-permute-start.41 = (bf16[256,2048]{1,0:T(8,128)(2,1)}, bf16[256,2048]{1,0:T(8,128)(2,1)}, u32[]{:S(2)}, u32[]{:S(2)}) collective-permute-start(bf16[256,2048]{1,0:T(8,128)(2,1)} %collective-permute-done.40), channel_id=1, source_target_pairs={{0,8},{1,9},{2,10},{3,11},{4,12},{5,13},{6,14},{7,15},{8,0},{9,1},... | collective-permute-start | bytes 3145736 | tf_op jit(solution)/shard_map/ppermute | solution.py:55
  489.5 76.6 %collective-permute-start.76 = (bf16[2048,688]{0,1:T(8,128)(2,1)}, bf16[2048,688]{0,1:T(8,128)(2,1)}, u32[]{:S(2)}, u32[]{:S(2)}) collective-permute-start(bf16[2048,688]{0,1:T(8,128)(2,1)} %convolution_convert_fusion.4), channel_id=1, source_target_pairs={{0,1},{1,0},{2,3},{3,2},{4,5},{5,4},{6,7},{7,6},{8,9},{9,8},{10,11... | collective-permute-start | bytes 8454152 | tf_op jit(solution)/shard_map/ppermute | solution.py:55
  520.9 91.9 %collective-permute-start.82 = (bf16[2048,688]{0,1:T(8,128)(2,1)}, bf16[2048,688]{0,1:T(8,128)(2,1)}, u32[]{:S(2)}, u32[]{:S(2)}) collective-permute-start(bf16[2048,688]{0,1:T(8,128)(2,1)} %convolution_convert_fusion.2), channel_id=1, source_target_pairs={{0,1},{1,0},{2,3},{3,2},{4,5},{5,4},{6,7},{7,6},{8,9},{9,8},{10,11... | collective-permute-start | bytes 8454152 | tf_op jit(solution)/shard_map/ppermute | solution.py:55
  528.9 144.4 %collective-permute-start.88 = (bf16[688,2048]{1,0:T(8,128)(2,1)}, bf16[688,2048]{1,0:T(8,128)(2,1)}, u32[]{:S(2)}, u32[]{:S(2)}) collective-permute-start(bf16[688,2048]{1,0:T(8,128)(2,1)} %convolution_convert_fusion.6), channel_id=1, source_target_pairs={{0,1},{1,0},{2,3},{3,2},{4,5},{5,4},{6,7},{7,6},{8,9},{9,8},{10,11... | collective-permute-start | bytes 8454152 | tf_op jit(solution)/shard_map/ppermute | solution.py:55
  550.0 211.7 %collective-permute-start.45 = (bf16[256,2048]{1,0:T(8,128)(2,1)}, bf16[256,2048]{1,0:T(8,128)(2,1)}, u32[]{:S(2)}, u32[]{:S(2)}) collective-permute-start(bf16[256,2048]{1,0:T(8,128)(2,1)} %fusion.34), channel_id=1, source_target_pairs={{0,2},{1,3},{2,0},{3,1},{4,6},{5,7},{6,4},{7,5},{8,10},{9,11},{10,... | collective-permute-start | bytes 3145736 | tf_op jit(solution)/shard_map/ppermute | solution.py:55
  558.2 123.5 %collective-permute-start.50 = (bf16[2,2,128,128]{3,2,1,0:T(8,128)(2,1)S(1)}, bf16[2,2,128,128]{3,2,1,0:T(8,128)(2,1)S(1)}, u32[]{:S(2)}, u32[]{:S(2)}) collective-permute-start(bf16[2,2,128,128]{3,2,1,0:T(8,128)(2,1)S(1)} %add_convert_fusion.20), channel_id=1, source_target_pairs={{16,0},{17,1},{18,2},{19,3},{20,4},{21,5},{22,6},{23,7},{24,8},{25... | collective-permute-start | bytes 393224 | tf_op jit(solution)/shard_map/ppermute | solution.py:55
  566.1 131.5 %collective-permute-start.49 = (bf16[2,2,128,128]{3,2,1,0:T(8,128)(2,1)}, bf16[2,2,128,128]{3,2,1,0:T(8,128)(2,1)S(1)}, u32[]{:S(2)}, u32[]{:S(2)}) collective-permute-start(bf16[2,2,128,128]{3,2,1,0:T(8,128)(2,1)} %add_convert_fusion.21), channel_id=1, source_target_pairs={{16,0},{17,1},{18,2},{19,3},{20,4},{21,5},{22,6},{23,7},{24,8},{25... | collective-permute-start | bytes 393224 | tf_op jit(solution)/shard_map/ppermute | solution.py:55
  612.9 152.9 %collective-permute-start.64 = (bf16[2048,256]{1,0:T(8,128)(2,1)}, bf16[2048,256]{1,0:T(8,128)(2,1)}, u32[]{:S(2)}, u32[]{:S(2)}) collective-permute-start(bf16[2048,256]{1,0:T(8,128)(2,1)} %convolution_convert_fusion.10), channel_id=1, source_target_pairs={{0,1},{1,0},{2,3},{3,2},{4,5},{5,4},{6,7},{7,6},{8,9},{9,8},{10,11... | collective-permute-start | bytes 3145736 | tf_op jit(solution)/shard_map/ppermute | solution.py:55
  673.3 97.4 %collective-permute-start.70 = (bf16[256,2048]{1,0:T(8,128)(2,1)}, bf16[256,2048]{1,0:T(8,128)(2,1)}, u32[]{:S(2)}, u32[]{:S(2)}) collective-permute-start(bf16[256,2048]{1,0:T(8,128)(2,1)} %convolution_convert_fusion.8), channel_id=1, source_target_pairs={{0,1},{1,0},{2,3},{3,2},{4,5},{5,4},{6,7},{7,6},{8,9},{9,8},{10,11... | collective-permute-start | bytes 3145736 | tf_op jit(solution)/shard_map/ppermute | solution.py:55
  682.4 91.3 %collective-permute-start.77 = (bf16[1024,688]{0,1:T(8,128)(2,1)}, bf16[1024,688]{0,1:T(8,128)(2,1)}, u32[]{:S(2)}, u32[]{:S(2)}) collective-permute-start(bf16[1024,688]{0,1:T(8,128)(2,1)} %broadcast_select_fusion.21), channel_id=1, source_target_pairs={{0,16},{1,17},{2,18},{3,19},{4,20},{5,21},{6,22},{7,23},{8,24},{9,... | collective-permute-start | bytes 4227080 | tf_op jit(solution)/shard_map/ppermute | solution.py:55
  697.6 77.4 %collective-permute-start.83 = (bf16[1024,688]{0,1:T(8,128)(2,1)}, bf16[1024,688]{0,1:T(8,128)(2,1)}, u32[]{:S(2)}, u32[]{:S(2)}) collective-permute-start(bf16[1024,688]{0,1:T(8,128)(2,1)} %broadcast_select_fusion.20), channel_id=1, source_target_pairs={{0,16},{1,17},{2,18},{3,19},{4,20},{5,21},{6,22},{7,23},{8,24},{9,... | collective-permute-start | bytes 4227080 | tf_op jit(solution)/shard_map/ppermute | solution.py:55
  765.8 98.9 %collective-permute-start.51 = (bf16[2,256,2048]{2,1,0:T(8,128)(2,1)S(1)}, bf16[2,256,2048]{2,1,0:T(8,128)(2,1)S(1)}, u32[]{:S(2)}, u32[]{:S(2)}) collective-permute-start(bf16[2,256,2048]{2,1,0:T(8,128)(2,1)S(1)} %slice_bitcast_fusion.1), channel_id=1, source_target_pairs={{0,8},{1,9},{2,10},{3,11},{4,12},{5,13},{6,14},{7,15},{8,0},{9,1},... | collective-permute-start | bytes 6291464 | tf_op jit(solution)/shard_map/ppermute | solution.py:55
  770.7 162.1 %collective-permute-start.58 = (bf16[2048,768]{1,0:T(8,128)(2,1)}, bf16[2048,768]{1,0:T(8,128)(2,1)S(1)}, u32[]{:S(2)}, u32[]{:S(2)}) collective-permute-start(bf16[2048,768]{1,0:T(8,128)(2,1)} %convolution_convert_fusion), channel_id=1, source_target_pairs={{0,1},{1,0},{2,3},{3,2},{4,5},{5,4},{6,7},{7,6},{8,9},{9,8},{10,11... | collective-permute-start | bytes 9437192 | tf_op jit(solution)/shard_map/ppermute | solution.py:55
  775.0 39.5 %collective-permute-start.71 = (bf16[256,1024]{1,0:T(8,128)(2,1)S(1)}, bf16[256,1024]{1,0:T(8,128)(2,1)S(1)}, u32[]{:S(2)}, u32[]{:S(2)}) collective-permute-start(bf16[256,1024]{1,0:T(8,128)(2,1)S(1)} %broadcast_select_fusion.40), channel_id=1, source_target_pairs={{0,16},{1,17},{2,18},{3,19},{4,20},{5,21},{6,22},{7,23},{8,24},{9,... | collective-permute-start | bytes 1572872 | tf_op jit(solution)/shard_map/ppermute | solution.py:55
  792.0 89.0 %collective-permute-start.78 = (bf16[1024,688]{0,1:T(8,128)(2,1)S(1)}, bf16[1024,688]{0,1:T(8,128)(2,1)S(1)}, u32[]{:S(2)}, u32[]{:S(2)}) collective-permute-start(bf16[1024,688]{0,1:T(8,128)(2,1)S(1)} %add_convert_fusion.11), channel_id=1, source_target_pairs={{8,12},{9,13},{10,14},{11,15},{12,8},{13,9},{14,10},{15,11},{24,28... | collective-permute-start | bytes 4227080 | tf_op jit(solution)/shard_map/ppermute | solution.py:55
  803.5 40.4 %collective-permute-start.66 = (bf16[1024,256]{1,0:T(8,128)(2,1)S(1)}, bf16[1024,256]{1,0:T(8,128)(2,1)S(1)}, u32[]{:S(2)}, u32[]{:S(2)}) collective-permute-start(bf16[1024,256]{1,0:T(8,128)(2,1)S(1)} %add_convert_fusion.17), channel_id=1, source_target_pairs={{8,12},{9,13},{10,14},{11,15},{12,8},{13,9},{14,10},{15,11},{24,28... | collective-permute-start | bytes 1572872 | tf_op jit(solution)/shard_map/ppermute | solution.py:55
  814.8 49.8 %collective-permute-start.72 = (bf16[256,1024]{1,0:T(8,128)(2,1)S(1)}, bf16[256,1024]{1,0:T(8,128)(2,1)S(1)}, u32[]{:S(2)}, u32[]{:S(2)}) collective-permute-start(bf16[256,1024]{1,0:T(8,128)(2,1)S(1)} %add_convert_fusion.16), channel_id=1, source_target_pairs={{8,12},{9,13},{10,14},{11,15},{12,8},{13,9},{14,10},{15,11},{24,28... | collective-permute-start | bytes 1572872 | tf_op jit(solution)/shard_map/ppermute | solution.py:55
  843.9 51.0 %collective-permute-start.84 = (bf16[1024,688]{0,1:T(8,128)(2,1)S(1)}, bf16[1024,688]{0,1:T(8,128)(2,1)S(1)}, u32[]{:S(2)}, u32[]{:S(2)}) collective-permute-start(bf16[1024,688]{0,1:T(8,128)(2,1)S(1)} %add_convert_fusion.10), channel_id=1, source_target_pairs={{8,12},{9,13},{10,14},{11,15},{12,8},{13,9},{14,10},{15,11},{24,28... | collective-permute-start | bytes 4227080 | tf_op jit(solution)/shard_map/ppermute | solution.py:55
  867.3 42.7 %collective-permute-start.90 = (bf16[688,1024]{1,0:T(8,128)(2,1)S(1)}, bf16[688,1024]{1,0:T(8,128)(2,1)S(1)}, u32[]{:S(2)}, u32[]{:S(2)}) collective-permute-start(bf16[688,1024]{1,0:T(8,128)(2,1)S(1)} %add_convert_fusion.9), channel_id=1, source_target_pairs={{8,12},{9,13},{10,14},{11,15},{12,8},{13,9},{14,10},{15,11},{24,28... | collective-permute-start | bytes 4227080 | tf_op jit(solution)/shard_map/ppermute | solution.py:55
  880.9 45.5 %collective-permute-start.52 = (bf16[256,2048]{1,0:T(8,128)(2,1)S(1)}, bf16[256,2048]{1,0:T(8,128)(2,1)S(1)}, u32[]{:S(2)}, u32[]{:S(2)}) collective-permute-start(bf16[256,2048]{1,0:T(8,128)(2,1)S(1)} %fusion.35), channel_id=1, source_target_pairs={{0,2},{1,3},{2,0},{3,1},{4,6},{5,7},{6,4},{7,5},{8,10},{9,11},{10,... | collective-permute-start | bytes 3145736 | tf_op jit(solution)/shard_map/ppermute | solution.py:55
  910.0 70.9 %collective-permute-start.79 = (bf16[512,688]{0,1:T(8,128)(2,1)S(1)}, bf16[512,688]{0,1:T(8,128)(2,1)S(1)}, u32[]{:S(2)}, u32[]{:S(2)}) collective-permute-start(bf16[512,688]{0,1:T(8,128)(2,1)S(1)} %broadcast_select_fusion.33), channel_id=1, source_target_pairs={{0,8},{1,9},{2,10},{3,11},{4,12},{5,13},{6,14},{7,15},{8,0},{9,1},... | collective-permute-start | bytes 2113544 | tf_op jit(solution)/shard_map/ppermute | solution.py:55
  910.3 72.7 %collective-permute-start.85 = (bf16[512,688]{0,1:T(8,128)(2,1)S(1)}, bf16[512,688]{0,1:T(8,128)(2,1)S(1)}, u32[]{:S(2)}, u32[]{:S(2)}) collective-permute-start(bf16[512,688]{0,1:T(8,128)(2,1)S(1)} %broadcast_select_fusion.32), channel_id=1, source_target_pairs={{0,8},{1,9},{2,10},{3,11},{4,12},{5,13},{6,14},{7,15},{8,0},{9,1},... | collective-permute-start | bytes 2113544 | tf_op jit(solution)/shard_map/ppermute | solution.py:55
  911.1 72.6 %collective-permute-start.91 = (bf16[688,512]{1,0:T(8,128)(2,1)S(1)}, bf16[688,512]{1,0:T(8,128)(2,1)S(1)}, u32[]{:S(2)}, u32[]{:S(2)}) collective-permute-start(bf16[688,512]{1,0:T(8,128)(2,1)S(1)} %broadcast_select_fusion.31), channel_id=1, source_target_pairs={{0,8},{1,9},{2,10},{3,11},{4,12},{5,13},{6,14},{7,15},{8,0},{9,1},... | collective-permute-start | bytes 2113544 | tf_op jit(solution)/shard_map/ppermute | solution.py:55
  944.4 56.8 %collective-permute-start.59 = (bf16[1024,768]{1,0:T(8,128)(2,1)S(1)}, bf16[1024,768]{1,0:T(8,128)(2,1)S(1)}, u32[]{:S(2)}, u32[]{:S(2)}) collective-permute-start(bf16[1024,768]{1,0:T(8,128)(2,1)S(1)} %broadcast_select_fusion.3), channel_id=1, source_target_pairs={{0,16},{1,17},{2,18},{3,19},{4,20},{5,21},{6,22},{7,23},{8,24},{9,... | collective-permute-start | bytes 4718600 | tf_op jit(solution)/shard_map/ppermute | solution.py:55
  945.6 35.3 %collective-permute-start.57 = (f32[19,256]{1,0:T(8,128)S(1)}, f32[19,256]{1,0:T(8,128)S(1)}, u32[]{:S(2)}, u32[]{:S(2)}) collective-permute-start(f32[19,256]{1,0:T(8,128)S(1)} %add.290), channel_id=1, source_target_pairs={{0,16},{1,17},{2,18},{3,19},{4,20},{5,21},{6,22},{7,23},{8,24},{9,... | collective-permute-start | bytes 58376 | tf_op jit(solution)/shard_map/ppermute | solution.py:55
  983.9 44.0 %collective-permute-start.92 = (bf16[688,512]{1,0:T(8,128)(2,1)S(1)}, bf16[688,512]{1,0:T(8,128)(2,1)S(1)}, u32[]{:S(2)}, u32[]{:S(2)}) collective-permute-start(bf16[688,512]{1,0:T(8,128)(2,1)S(1)} %add_convert_fusion.13), channel_id=1, source_target_pairs={{0,16},{1,17},{2,18},{3,19},{4,20},{5,21},{6,22},{7,23},{8,24},{9,... | collective-permute-start | bytes 2113544 | tf_op jit(solution)/shard_map/ppermute | solution.py:55
  1001.8 38.4 %collective-permute-start.60 = (bf16[1024,768]{1,0:T(8,128)(2,1)S(1)}, bf16[1024,768]{1,0:T(8,128)(2,1)S(1)}, u32[]{:S(2)}, u32[]{:S(2)}) collective-permute-start(bf16[1024,768]{1,0:T(8,128)(2,1)S(1)} %add_convert_fusion.8), channel_id=1, source_target_pairs={{8,12},{9,13},{10,14},{11,15},{12,8},{13,9},{14,10},{15,11},{24,28... | collective-permute-start | bytes 4718600 | tf_op jit(solution)/shard_map/ppermute | solution.py:55
  (199 other events, 3575.2 us)
